TPU v7x, 512 devices: a whole 4x8x8 slice. The times are simulated.
512 devices in a mesh: row: 8 (over z_lo, core), bulk: 64 (over z_hi, x, y).
Axes of the slice: x: 4, y: 8, z: 8 (z_hi: 2, z_lo: 4; z = z_hi * 4 + z_lo), core: 2. Of those that a mesh axis runs over, the one named last changes fastest.
Arguments:
- residual_in: float32 [2048, 65536], P('row', 'bulk'), may hold values from -6 to 6
- amplitudes: float32 [2048, 2048], P('row', 'bulk'), may hold values from -6 to 6
- integral_tiles: float32 [4096, 128, 128], P('bulk', 'row'), may hold values from -0.1875 to 0.1875
- tile_reader: int32 [4096, 1], P('bulk'), may hold values from 0 to 63; in each aligned block of 64 rows (0 to 63, 64 to 127, ...) at most 2 rows name the same one
- tile_k: int32 [4096], P('bulk'), may hold values from 0 to 15
- tile_column: int32 [4096], P('bulk'), may hold values from 0 to 7
Outputs:
- residual_out: float32 [2048, 65536], P('row', 'bulk')
Inputs may be any that keep to these rules, and one draw needn't show every extreme that they name: `tile_reader`: among the 64 tiles stored on one index of bulk (aligned blocks of 64 entries), at most 2 name the same reader; some block has exactly 2 for some reader.
All inputs are finite; a program needn't handle non-finite values.
Results may differ from a plain program's by a relative error of at most 0.0003.
Values sent between devices are 32-bit elements; how exact they have to be, the bound alone decides.
A program may use at most 64 MiB of HBM per device.

v0:
```python
import jax
import jax.numpy as jnp
from jax import lax
from jax.sharding import PartitionSpec as P

KT = 16
CT = 8
SLOT = 2


def bucket_slots(tile_reader, tile_k, tile_column, targets, slots):
    readers = tile_reader[:, 0]
    matches = (readers[:, None] == jnp.arange(targets, dtype=jnp.int32)[None, :]).astype(jnp.int32)
    ordinal = jnp.cumsum(matches, axis=0) - matches
    position = jnp.sum(ordinal * matches, axis=1)
    select = matches.T[:, None, :] * (
        position[None, None, :] == jnp.arange(slots, dtype=jnp.int32)[None, :, None]
    ).astype(jnp.int32)
    filled = jnp.sum(select, axis=2)
    slot_tile = jnp.sum(select * tile_k[None, None, :], axis=2) + filled - 1
    slot_column = jnp.sum(select * tile_column[None, None, :], axis=2) + filled - 1
    return (select.astype(jnp.float32), slot_tile, slot_column)


def pair_table(slot_tile, slot_column, tiles_count, column_count):
    tile_hot = (slot_tile[:, None] == jnp.arange(tiles_count, dtype=jnp.int32)[None, :]).astype(
        jnp.float32
    )
    column_hot = (
        slot_column[:, None] == jnp.arange(column_count, dtype=jnp.int32)[None, :]
    ).astype(jnp.float32)
    return (tile_hot[:, :, None] * column_hot[:, None, :]).reshape(
        slot_tile.shape[0], tiles_count * column_count
    )


def place_rows(table, portion, tiles_count, column_count):
    width = portion.shape[2]
    height = portion.shape[1]
    placed = jnp.dot(
        table.T, portion.reshape(portion.shape[0], height * width), precision=lax.Precision.HIGHEST
    )
    placed = placed.reshape(tiles_count, column_count, height, width).transpose(0, 2, 1, 3)
    return placed


def local(residual_in, amplitudes, integral_tiles, tile_reader, tile_k, tile_column):
    targets = lax.axis_size("bulk")
    select, slot_tile, slot_column = bucket_slots(tile_reader, tile_k, tile_column, targets, SLOT)
    width = integral_tiles.shape[2]
    whole_tiles = lax.all_gather(integral_tiles, "row", axis=1, tiled=True)
    outgoing = jnp.einsum("dsj,jpq->dspq", select, whole_tiles, precision=lax.Precision.HIGHEST)
    arrived, arrived_tile, arrived_column = (
        lax.all_to_all(outgoing, "bulk", split_axis=0, concat_axis=0, tiled=True),
        lax.all_to_all(slot_tile, "bulk", split_axis=0, concat_axis=0, tiled=True),
        lax.all_to_all(slot_column, "bulk", split_axis=0, concat_axis=0, tiled=True),
    )
    arrived = arrived.reshape(targets * SLOT, width, width)
    table = pair_table(arrived_tile.reshape(-1), arrived_column.reshape(-1), KT, CT)
    assembled = place_rows(table, arrived, KT, CT)
    dense_block = assembled.reshape(KT * width, CT * width)
    return residual_in + jnp.dot(
        lax.all_gather(amplitudes, "bulk", axis=1, tiled=True),
        dense_block,
        precision=lax.Precision.HIGHEST,
    )


def solution(mesh):
    placed = (
        P("row", "bulk"),
        P("row", "bulk"),
        P("bulk", "row", None),
        P("bulk", None),
        P("bulk"),
        P("bulk"),
    )
    return jax.shard_map(
        local, mesh=mesh, in_specs=placed, out_specs=P("row", "bulk"), check_vma=False
    )
```

profile of v0, /device:TPU:6, one launch (start us, length us, event | category | flops | bytes accessed | tf_op | source)
XLA Modules:
  0.0 432.4 jit_solution(5636964937242267138)
XLA Ops:
  7.4 0.0 all-gather.3.cloned.1.call-start
  7.4 2.0 copy.21
  9.4 0.0 all-gather.3.cloned.1.call-update
  9.4 0.8 fusion.23
  10.2 0.1 reduce_window_sum.11
  10.3 0.8 select_reduce_fusion
  11.2 0.9 fusion.11
  12.0 0.7 copy.19
  12.7 19.1 %all-to-all-start = ((s32[64,1,2]{2,1,0:T(1,128)}), s32[64,1,2]{2,1,0:T(1,128)S(1)}, u32[]{:S(2)}, u32[]{:S(2)}) async-start(s32[64,1,2]{2,1,0:T(1,128)} %copy.19), calls=%async_computation | async-start | bytes 65536 | tf_op jit(solution)/shard_map/all_to_all | solution.py:55
  31.8 0.7 copy.20
  32.5 12.2 %all-to-all-done = s32[64,1,2]{2,1,0:T(1,128)S(1)} async-done(((s32[64,1,2]{2,1,0:T(1,128)}), s32[64,1,2]{2,1,0:T(1,128)S(1)}, u32[]{:S(2)}, u32[]{:S(2)}) %all-to-all-start) | async-done | bytes 544 | tf_op jit(solution)/shard_map/all_to_all | solution.py:55
  44.7 6.0 %all-to-all-start.1 = ((s32[64,1,2]{2,1,0:T(1,128)}), s32[64,1,2]{2,1,0:T(1,128)S(1)}, u32[]{:S(2)}, u32[]{:S(2)}) async-start(s32[64,1,2]{2,1,0:T(1,128)} %copy.20), calls=%async_computation.1 | async-start | bytes 65536 | tf_op jit(solution)/shard_map/all_to_all | solution.py:56
  50.8 23.4 %all-gather.3.cloned.1.call-done = f32[64,128,128]{2,0,1:T(8,128)} async-done(((f32[64,16,128]{2,0,1:T(8,128)}), f32[64,128,128]{2,0,1:T(8,128)}) %all-gather.3.cloned.1.call-update) | async-done | bytes 4194320 | tf_op jit(solution)/shard_map/all_gather | solution.py:51
  74.1 8.7 %fusion.3 = f32[64,2,128,128]{3,0,2,1:T(8,128)S(1)} fusion(f32[64,128,128]{2,0,1:T(8,128)} %all-gather.3.cloned.1.call-done, s32[2,64]{1,0:T(2,128)S(1)} %compare_convert_fusion, s32[64,64]{1,0:T(8,128)S(1)} %get-tuple-element.10), kind=kOutput, calls=%fused_computation.4 | convolution fusion | flops 1610629120 | bytes 12599808 | tf_op jit(solution)/shard_map/dsj,jpq->dspq/dot_general | solution.py:52
  82.9 8.1 %copy.22 = f32[64,2,128,128]{3,2,1,0:T(8,128)} copy(f32[64,2,128,128]{3,0,2,1:T(8,128)S(1)} %fusion.3) | data formatting | bytes 16777216 | tf_op jit(solution)/shard_map/dsj,jpq->dspq/dot_general | solution.py:52
  90.9 0.0 copy-start
  90.9 0.0 all-to-all-done.1
  90.9 13.5 %all-to-all-start.2 = ((f32[64,2,128,128]{3,2,1,0:T(8,128)}), f32[64,2,128,128]{3,2,1,0:T(8,128)}, u32[]{:S(2)}, u32[]{:S(2)}) async-start(f32[64,2,128,128]{3,2,1,0:T(8,128)} %copy.22), calls=%async_computation.2 | async-start | bytes 16777216 | tf_op jit(solution)/shard_map/all_to_all | solution.py:54
  104.4 0.0 all-gather.5.cloned.1.call-start
  104.5 0.5 all-gather.5.cloned.1.call-update
  105.0 0.0 copy-done
  105.0 0.3 copy.24
  105.3 0.5 broadcast.89
  105.8 0.7 reduce.7
  106.6 0.1 eq.92
  106.7 0.7 reduce.6
  107.5 0.1 eq.96
  107.6 237.7 %all-to-all-done.2 = f32[64,2,128,128]{3,2,1,0:T(8,128)} async-done(((f32[64,2,128,128]{3,2,1,0:T(8,128)}), f32[64,2,128,128]{3,2,1,0:T(8,128)}, u32[]{:S(2)}, u32[]{:S(2)}) %all-to-all-start.2) | async-done | bytes 8388640 | tf_op jit(solution)/shard_map/all_to_all | solution.py:54
  345.3 13.1 %copy.39 = f32[16,8,128,128]{3,1,2,0:T(8,128)} copy(f32[16,8,128,128]{3,2,1,0:T(8,128)} %bitcast.23) | data formatting | bytes 16777216
  358.5 9.0 %copy.23 = f32[16384,128]{1,0:T(8,128)} copy(f32[16384,128]{0,1:T(8,128)} %bitcast.53) | data formatting | bytes 16777216 | tf_op jit(solution)/shard_map/dot_general | solution.py:40
  367.5 12.1 %fusion.15 = f32[16,8,128,128]{3,1,2,0:T(8,128)} fusion(f32[128,128,128,1]{2,1,0,3:T(8,128)} %bitcast.52, f32[128,8]{0,1:T(8,128)S(1)} %fusion.25, f32[128,16]{0,1:T(8,128)S(1)} %fusion.24), kind=kOutput, calls=%fused_computation.15 | convolution fusion | flops 3221241856 | bytes 16789504 | tf_op jit(solution)/shard_map/dot_general | solution.py:40
  379.6 27.1 %all-gather.5.cloned.1.call-done = f32[256,2048]{0,1:T(8,128)} async-done(((f32[256,32]{0,1:T(8,128)}), f32[256,2048]{0,1:T(8,128)}) %all-gather.5.cloned.1.call-update) | async-done | bytes 2097168 | tf_op jit(solution)/shard_map/all_gather | solution.py:63
  406.6 17.1 %fusion.8 = f32[256,1024]{0,1:T(8,128)S(1)} fusion(f32[256,1024]{0,1:T(8,128)S(1)} %copy.24, f32[256,2048]{0,1:T(8,128)} %all-gather.5.cloned.1.call-done, f32[256,8,8,128]{3,2,1,0:T(8,128)} %bitcast.51), kind=kOutput, calls=%fused_computation.7 | convolution fusion | flops 6442713088 | bytes 12582912 | tf_op jit(solution)/shard_map/dot_general | solution.py:62
  423.7 1.3 copy.25
  (4 shorter events, 0.0 us)
Async XLA Ops:
  7.4 66.7 %all-gather.3.cloned.1.call-start = ((), (), s32[]{:S(2)}) async-start(), calls=%async_computation.3 | async-start | bytes 4718592 | tf_op jit(solution)/shard_map/all_gather | solution.py:51
  12.7 32.0 %all-to-all-start = ((s32[64,1,2]{2,1,0:T(1,128)}), s32[64,1,2]{2,1,0:T(1,128)S(1)}, u32[]{:S(2)}, u32[]{:S(2)}) async-start(s32[64,1,2]{2,1,0:T(1,128)} %copy.19), calls=%async_computation | async-start | bytes 65536 | tf_op jit(solution)/shard_map/all_to_all | solution.py:55
  44.7 46.2 %all-to-all-start.1 = ((s32[64,1,2]{2,1,0:T(1,128)}), s32[64,1,2]{2,1,0:T(1,128)S(1)}, u32[]{:S(2)}, u32[]{:S(2)}) async-start(s32[64,1,2]{2,1,0:T(1,128)} %copy.20), calls=%async_computation.1 | async-start | bytes 65536 | tf_op jit(solution)/shard_map/all_to_all | solution.py:56
  90.9 14.1 %copy-start = (f32[256,1024]{1,0:T(8,128)S(1)}, f32[256,1024]{1,0:T(8,128)}, u32[]{:S(2)}) copy-start(f32[256,1024]{1,0:T(8,128)} %param.6) | copy-start | bytes 3145732
  90.9 254.4 %all-to-all-start.2 = ((f32[64,2,128,128]{3,2,1,0:T(8,128)}), f32[64,2,128,128]{3,2,1,0:T(8,128)}, u32[]{:S(2)}, u32[]{:S(2)}) async-start(f32[64,2,128,128]{3,2,1,0:T(8,128)} %copy.22), calls=%async_computation.2 | async-start | bytes 16777216 | tf_op jit(solution)/shard_map/all_to_all | solution.py:54
  104.4 302.2 %all-gather.5.cloned.1.call-start = ((), (), s32[]{:S(2)}) async-start(), calls=%async_computation.4 | async-start | bytes 2129920 | tf_op jit(solution)/shard_map/all_gather | solution.py:63
Sparse Core Ops, SparseCore 0:
  10.3 63.7 all-gather.2
Sparse Core Ops, SparseCore 1:
  109.4 297.2 all-gather.4
where the time goes:
time: 433 us; the launch traced here: 432 us
  waiting for transfers between devices  301 us (70%)
  starting transfers between devices  38.6 us (9%)
  matrix products  37.9 us (9%)
  local copies, waits for them, and re-layouts  36.1 us (8%)
  between operations  15 us (3%)
    all_to_all x1, waiting for transfers between devices, local(): lax.all_to_all(outgoing, 'bulk', split_axis=0, concat_axis=0, tiled=True)  238 us
    all_gather x1, waiting for transfers between devices, local(): lax.all_gather(amplitudes, 'bulk', axis=1, tiled=True)  27.1 us
    all_gather x1, waiting for transfers between devices, local(): whole_tiles = lax.all_gather(integral_tiles, 'row', axis=1, tiled=True)  23.4 us
    all_to_all x1, starting transfers between devices, local(): lax.all_to_all(slot_tile, 'bulk', split_axis=0, concat_axis=0, tiled=True)  19.1 us
    dot_general x1, matrix products, local(): jnp.dot(lax.all_gather(amplitudes, 'bulk', axis=1, tiled=True), dense_blo...  17.1 us
    unnamed x5, local copies, waits for them, and re-layouts  15.5 us
    all_to_all x1, starting transfers between devices, local(): lax.all_to_all(outgoing, 'bulk', split_axis=0, concat_axis=0, tiled=True)  13.5 us
    all_to_all x1, waiting for transfers between devices, local(): lax.all_to_all(slot_tile, 'bulk', split_axis=0, concat_axis=0, tiled=True)  12.2 us
  transfers between devices with their start and end apart: 5, of which 4 were waited for; matrix products, arithmetic and copies ran while one was open for 13% of the time, Pallas kernels for 0%

commit v1 on v0

v1 whole, which is shorter than its diff:
```python
import jax
import jax.numpy as jnp
import numpy as np
from jax import lax
from jax.sharding import Mesh, PartitionSpec as P

KT = 16
CT = 8
SLOT = 2


def bucket_slots(tile_reader, tile_k, tile_column, targets, slots):
    readers = tile_reader[:, 0]
    matches = (readers[:, None] == jnp.arange(targets, dtype=jnp.int32)[None, :]).astype(jnp.int32)
    ordinal = jnp.cumsum(matches, axis=0) - matches
    position = jnp.sum(ordinal * matches, axis=1)
    select = matches.T[:, None, :] * (
        position[None, None, :] == jnp.arange(slots, dtype=jnp.int32)[None, :, None]
    ).astype(jnp.int32)
    filled = jnp.sum(select, axis=2)
    local_index = jnp.sum(select * jnp.arange(readers.shape[0], dtype=jnp.int32)[None, None, :], axis=2)
    slot_tile = jnp.sum(select * tile_k[None, None, :], axis=2) + filled - 1
    slot_column = jnp.sum(select * tile_column[None, None, :], axis=2) + filled - 1
    return filled, local_index, slot_tile, slot_column


def local(residual_in, amplitudes, integral_tiles, tile_reader, tile_k, tile_column):
    targets = lax.axis_size("bulk")
    height, width = integral_tiles.shape[1], integral_tiles.shape[2]
    filled, local_index, slot_tile, slot_column = bucket_slots(
        tile_reader, tile_k, tile_column, targets, SLOT
    )
    picked = jnp.take(integral_tiles, local_index.reshape(-1), axis=0)
    picked = jnp.where(filled.reshape(-1)[:, None, None] > 0, picked, 0.0)
    outgoing = picked.reshape(targets, SLOT, height, width)
    arrived, arrived_tile, arrived_column = (
        lax.all_to_all(outgoing, "bulk", split_axis=0, concat_axis=0, tiled=True),
        lax.all_to_all(slot_tile, "bulk", split_axis=0, concat_axis=0, tiled=True),
        lax.all_to_all(slot_column, "bulk", split_axis=0, concat_axis=0, tiled=True),
    )
    arrived = arrived.reshape(targets * SLOT, height * width)
    position = arrived_tile.reshape(-1) * CT + arrived_column.reshape(-1)
    table = (position[None, :] == jnp.arange(KT * CT, dtype=jnp.int32)[:, None]).astype(jnp.float32)
    placed = jnp.dot(table, arrived, precision=lax.Precision.HIGHEST)
    placed = placed.reshape(KT, CT, height, width).transpose(0, 2, 1, 3).reshape(KT * height, CT * width)
    gathered = lax.all_gather(placed, "zl", axis=0, tiled=False)
    gathered = lax.all_gather(gathered, "core", axis=1, tiled=False)
    dense = gathered.reshape(-1, CT * width)
    amps = lax.all_gather(amplitudes, "bulk", axis=1, tiled=True)
    rows = amps.shape[0]
    groups = gathered.shape[0] * gathered.shape[1]
    amps = amps.reshape(rows, KT, groups, height).transpose(0, 2, 1, 3).reshape(rows, -1)
    return residual_in + jnp.dot(amps, dense, precision=lax.Precision.HIGHEST)


def solution(mesh):
    row_size = mesh.shape["row"]
    devices = np.asarray(mesh.devices).reshape(row_size // 2, 2, mesh.shape["bulk"])
    inner = Mesh(devices, ("zl", "core", "bulk"))
    row = ("zl", "core")
    placed = (
        P(row, "bulk"),
        P(row, "bulk"),
        P("bulk", row, None),
        P("bulk", None),
        P("bulk"),
        P("bulk"),
    )
    return jax.shard_map(
        local, mesh=inner, in_specs=placed, out_specs=P(row, "bulk"), check_vma=False
    )
```

time: 433 us -> 377 us (0.87)
  local copies, waits for them, and re-layouts: 36.1 us -> 10.2 us
  matrix products: 37.9 us -> 17.2 us
  starting transfers between devices: 38.6 us -> 31.5 us
    all_to_all x1, waiting for transfers between devices: 238 us -> 30.3 us  [local(): lax.all_to_all(outgoing, 'bulk', split_axis=0, concat_axis=0, tiled=True)]
    all_gather x2 -> x3, waiting for transfers between devices: 50.4 us -> 244 us  [the longest x1 142 us: local(): amps = lax.all_gather(amplitudes, 'bulk', axis=1, tiled=True)]
    dot_general x3 -> x2, matrix products: 37.9 us -> 17.2 us  [the longest x1 16.5 us: local(): return residual_in + jnp.dot(amps, dense, precision=lax.Precision.HIGHEST)]
    dot_general x2 -> x1, local copies, waits for them, and re-layouts: 17.1 us -> 0.32 us  [local(): placed = jnp.dot(table, arrived, precision=lax.Precision.HIGHEST)]
    unnamed x5 -> x6, local copies, waits for them, and re-layouts: 15.5 us -> 1.66 us
    all_to_all x1, waiting for transfers between devices: 0.01 us -> 11.6 us  [local(): lax.all_to_all(slot_column, 'bulk', split_axis=0, concat_axis=0, tiled=True)]
    all_to_all x1, starting transfers between devices: 13.5 us -> 6.15 us  [local(): lax.all_to_all(outgoing, 'bulk', split_axis=0, concat_axis=0, tiled=True)]
  transfers between devices with their start and end apart: 5 -> 6, of which waited for: 4 -> 6; matrix products, arithmetic and copies ran while one was open for 13% -> 2% of each run, Pallas kernels for 0% -> 0%
where the time goes in v1:
time: 377 us; the launch traced here: 374 us
  waiting for transfers between devices  297 us (79%)
  starting transfers between devices  31.5 us (8%)
  matrix products  17.2 us (5%)
  between operations  13.3 us (4%)
  local copies, waits for them, and re-layouts  10.2 us (3%)
  other arithmetic  4.08 us (1%)
    all_gather x1, waiting for transfers between devices, local(): amps = lax.all_gather(amplitudes, 'bulk', axis=1, tiled=True)  142 us
    all_gather x1, waiting for transfers between devices, local(): gathered = lax.all_gather(placed, 'zl', axis=0, tiled=False)  80 us
    all_to_all x1, waiting for transfers between devices, local(): lax.all_to_all(outgoing, 'bulk', split_axis=0, concat_axis=0, tiled=True)  30.3 us
    all_gather x1, waiting for transfers between devices, local(): gathered = lax.all_gather(gathered, 'core', axis=1, tiled=False)  21.5 us
    all_to_all x1, starting transfers between devices, local(): lax.all_to_all(slot_tile, 'bulk', split_axis=0, concat_axis=0, tiled=True)  19.1 us
    dot_general x1, matrix products, local(): return residual_in + jnp.dot(amps, dense, precision=lax.Precision.HIGHEST)  16.5 us
    all_to_all x1, waiting for transfers between devices, local(): lax.all_to_all(slot_column, 'bulk', split_axis=0, concat_axis=0, tiled=True)  11.6 us
    all_to_all x1, waiting for transfers between devices, local(): lax.all_to_all(slot_tile, 'bulk', split_axis=0, concat_axis=0, tiled=True)  10.8 us
  transfers between devices with their start and end apart: 6, of which 6 were waited for; matrix products, arithmetic and copies ran while one was open for 2% of the time, Pallas kernels for 0%

profile of v1, /device:TPU:6, one launch (start us, length us, event | category | flops | bytes accessed | tf_op | source)
XLA Modules:
  0.0 373.8 jit_solution(10225368570562144597)
XLA Ops:
  6.5 0.0 copy-start
  6.5 0.8 fusion.9
  7.3 0.1 reduce_window_sum.11
  7.4 0.8 select_reduce_fusion
  8.3 0.9 fusion.1
  9.2 0.7 copy.34
  9.9 19.1 %all-to-all-start = ((s32[64,1,2]{2,1,0:T(1,128)}), s32[64,1,2]{2,1,0:T(1,128)S(1)}, u32[]{:S(2)}, u32[]{:S(2)}) async-start(s32[64,1,2]{2,1,0:T(1,128)} %copy.34), calls=%async_computation | async-start | bytes 65536 | tf_op jit(solution)/shard_map/all_to_all | solution.py:38
  29.0 0.1 copy.38
  29.1 0.1 reshape.184
  29.3 0.7 copy.35
  30.0 0.1 copy.36
  30.1 0.1 copy.37
  30.2 0.0 copy-done
  30.2 0.8 gather_fusion
  31.0 10.8 %all-to-all-done = s32[64,1,2]{2,1,0:T(1,128)S(1)} async-done(((s32[64,1,2]{2,1,0:T(1,128)}), s32[64,1,2]{2,1,0:T(1,128)S(1)}, u32[]{:S(2)}, u32[]{:S(2)}) %all-to-all-start) | async-done | bytes 544 | tf_op jit(solution)/shard_map/all_to_all | solution.py:38
  41.8 6.0 %all-to-all-start.1 = ((s32[64,1,2]{2,1,0:T(1,128)}), s32[64,1,2]{2,1,0:T(1,128)S(1)}, u32[]{:S(2)}, u32[]{:S(2)}) async-start(s32[64,1,2]{2,1,0:T(1,128)} %copy.35), calls=%async_computation.1 | async-start | bytes 65536 | tf_op jit(solution)/shard_map/all_to_all | solution.py:39
  47.8 1.3 select_select_fusion
  49.1 11.6 %all-to-all-done.1 = s32[64,1,2]{2,1,0:T(1,128)S(1)} async-done(((s32[64,1,2]{2,1,0:T(1,128)}), s32[64,1,2]{2,1,0:T(1,128)S(1)}, u32[]{:S(2)}, u32[]{:S(2)}) %all-to-all-start.1) | async-done | bytes 544 | tf_op jit(solution)/shard_map/all_to_all | solution.py:39
  60.7 6.1 %all-to-all-start.2 = ((f32[64,2,16,128]{3,2,1,0:T(8,128)}), f32[64,2,16,128]{3,2,1,0:T(8,128)S(1)}, u32[]{:S(2)}, u32[]{:S(2)}) async-start(f32[64,2,16,128]{3,2,1,0:T(8,128)} %select_select_fusion), calls=%async_computation.2 | async-start | bytes 2097152 | tf_op jit(solution)/shard_map/all_to_all | solution.py:37
  66.9 0.0 all-gather.5.cloned.1.call-start
  67.0 0.1 add_reduce_fusion
  67.1 0.1 add.82
  67.2 30.3 %all-to-all-done.2 = f32[64,2,16,128]{3,2,1,0:T(8,128)S(1)} async-done(((f32[64,2,16,128]{3,2,1,0:T(8,128)}), f32[64,2,16,128]{3,2,1,0:T(8,128)S(1)}, u32[]{:S(2)}, u32[]{:S(2)}) %all-to-all-start.2) | async-done | bytes 1048608 | tf_op jit(solution)/shard_map/all_to_all | solution.py:37
  97.5 0.3 copy.46
  97.9 0.3 copy.39
  98.2 0.7 convolution_bitcast_fusion.1
  98.9 0.0 copy-start.1
  98.9 1.1 all_gather_reshape.3
  100.0 0.0 all-gather.5.cloned.1.call-update
  100.1 0.0 all-gather.7.cloned.1.call-start
  100.1 0.7 all-gather.7.cloned.1.call-update
  100.8 0.2 all-gather.9.cloned.1.call-start
  101.0 80.0 %all-gather.5.cloned.1.call-done = f32[4,256,1024]{2,1,0:T(8,128)} async-done(((f32[1,256,1024]{2,1,0:T(8,128)}), f32[4,256,1024]{2,1,0:T(8,128)}) %all-gather.5.cloned.1.call-update) | async-done | bytes 4194320 | tf_op jit(solution)/shard_map/all_gather | solution.py:46
  181.1 0.0 all-gather.9.cloned.1.call-update
  181.1 0.0 copy-done.1
  181.1 1.3 copy.41
  182.4 142.5 %all-gather.7.cloned.1.call-done = f32[256,2048]{0,1:T(8,128)} async-done(((f32[256,32]{0,1:T(8,128)}), f32[256,2048]{0,1:T(8,128)}) %all-gather.7.cloned.1.call-update) | async-done | bytes 2097168 | tf_op jit(solution)/shard_map/all_gather | solution.py:49
  324.9 1.8 copy.40
  326.7 21.5 %all-gather.9.cloned.1.call-done = f32[4,512,1024]{2,1,0:T(8,128)} async-done(((f32[4,256,1024]{2,1,0:T(8,128)}), f32[4,512,1024]{2,1,0:T(8,128)}) %all-gather.9.cloned.1.call-update) | async-done | bytes 8388624 | tf_op jit(solution)/shard_map/all_gather | solution.py:47
  348.2 16.5 %fusion = f32[256,1024]{0,1:T(8,128)} fusion(f32[256,1024]{0,1:T(8,128)} %copy.41, f32[2048,1024]{1,0:T(8,128)} %bitcast.40, f32[256,2048]{0,1:T(8,128)S(1)} %bitcast.41), kind=kOutput, calls=%fused_computation.3 | convolution fusion | flops 6442713088 | bytes 12582912 | tf_op jit(solution)/shard_map/dot_general | solution.py:53
  364.7 2.5 copy.42
  (6 shorter events, 0.0 us)
Async XLA Ops:
  6.5 23.7 %copy-start = (f32[64,16,128]{2,1,0:T(8,128)S(1)}, f32[64,16,128]{2,1,0:T(8,128)}, u32[]{:S(2)}) copy-start(f32[64,16,128]{2,1,0:T(8,128)} %param.8) | copy-start | bytes 1572868
  9.9 31.9 %all-to-all-start = ((s32[64,1,2]{2,1,0:T(1,128)}), s32[64,1,2]{2,1,0:T(1,128)S(1)}, u32[]{:S(2)}, u32[]{:S(2)}) async-start(s32[64,1,2]{2,1,0:T(1,128)} %copy.34), calls=%async_computation | async-start | bytes 65536 | tf_op jit(solution)/shard_map/all_to_all | solution.py:38
  41.8 18.9 %all-to-all-start.1 = ((s32[64,1,2]{2,1,0:T(1,128)}), s32[64,1,2]{2,1,0:T(1,128)S(1)}, u32[]{:S(2)}, u32[]{:S(2)}) async-start(s32[64,1,2]{2,1,0:T(1,128)} %copy.35), calls=%async_computation.1 | async-start | bytes 65536 | tf_op jit(solution)/shard_map/all_to_all | solution.py:39
  60.7 36.8 %all-to-all-start.2 = ((f32[64,2,16,128]{3,2,1,0:T(8,128)}), f32[64,2,16,128]{3,2,1,0:T(8,128)S(1)}, u32[]{:S(2)}, u32[]{:S(2)}) async-start(f32[64,2,16,128]{3,2,1,0:T(8,128)} %select_select_fusion), calls=%async_computation.2 | async-start | bytes 2097152 | tf_op jit(solution)/shard_map/all_to_all | solution.py:37
  66.9 114.2 %all-gather.5.cloned.1.call-start = ((), (), s32[]{:S(2)}) async-start(), calls=%async_computation.3 | async-start | bytes 5242880 | tf_op jit(solution)/shard_map/all_gather | solution.py:46
  98.9 82.2 %copy-start.1 = (f32[256,1024]{1,0:T(8,128)S(1)}, f32[256,1024]{1,0:T(8,128)}, u32[]{:S(2)}) copy-start(f32[256,1024]{1,0:T(8,128)} %param.6) | copy-start | bytes 3145732
  100.1 224.8 %all-gather.7.cloned.1.call-start = ((), (), s32[]{:S(2)}) async-start(), calls=%async_computation.4 | async-start | bytes 2129920 | tf_op jit(solution)/shard_map/all_gather | solution.py:49
  100.8 247.4 %all-gather.9.cloned.1.call-start = ((), (), s32[]{:S(2)}) async-start(), calls=%async_computation.5 | async-start | bytes 12582912 | tf_op jit(solution)/shard_map/all_gather | solution.py:47
Sparse Core Ops, SparseCore 0:
  100.2 80.8 all-gather.4
  185.6 139.2 all-gather.6
  327.0 21.1 all-gather.8

commit v2 on v1

v2 whole, which is shorter than its diff:
```python
import functools

import jax
import jax.numpy as jnp
import numpy as np
from jax import lax
from jax.experimental import pallas as pl
from jax.experimental.pallas import tpu as pltpu
from jax.sharding import Mesh, PartitionSpec as P

MESH = pl.DeviceIdType.MESH

KT = 16
CT = 8
SLOT = 2


def bucket_slots(tile_reader, tile_k, tile_column, targets, slots):
    readers = tile_reader[:, 0]
    matches = (readers[:, None] == jnp.arange(targets, dtype=jnp.int32)[None, :]).astype(jnp.int32)
    ordinal = jnp.cumsum(matches, axis=0) - matches
    position = jnp.sum(ordinal * matches, axis=1)
    select = matches.T[:, None, :] * (
        position[None, None, :] == jnp.arange(slots, dtype=jnp.int32)[None, :, None]
    ).astype(jnp.int32)
    filled = jnp.sum(select, axis=2)
    local_index = jnp.sum(select * jnp.arange(readers.shape[0], dtype=jnp.int32)[None, None, :], axis=2)
    slot_position = jnp.sum(select * (tile_k * CT + tile_column)[None, None, :], axis=2) + filled - 1
    return filled, local_index, slot_position


def gather_kernel(nz, src_ref, out_ref, local_sem, send_sem, recv_sem):
    zl = lax.axis_index("zl")
    c = lax.axis_index("core")
    b = lax.axis_index("bulk")
    partner = (zl, 1 - c, b)
    left = (zl - 1, c, b)
    right = (zl + 1, c, b)
    has_left = zl > 0
    has_right = zl < nz - 1
    own = zl * 2 + c

    barrier = pltpu.get_barrier_semaphore()
    pl.semaphore_signal(barrier, 1, device_id=partner, device_id_type=MESH)

    @pl.when(has_left)
    def _():
        pl.semaphore_signal(barrier, 1, device_id=left, device_id_type=MESH)

    @pl.when(has_right)
    def _():
        pl.semaphore_signal(barrier, 1, device_id=right, device_id_type=MESH)

    peers = 1 + has_left.astype(jnp.int32) + has_right.astype(jnp.int32)
    pl.semaphore_wait(barrier, peers)

    def copy(src, slot, kind, dev):
        return pltpu.make_async_remote_copy(
            src_ref=src,
            dst_ref=out_ref.at[slot],
            send_sem=send_sem.at[slot, kind],
            recv_sem=recv_sem.at[slot],
            device_id=dev,
            device_id_type=MESH,
        )

    mine = pltpu.make_async_copy(src_ref, out_ref.at[own], local_sem)
    mine.start()
    copy(src_ref, own, 0, partner).start()

    @pl.when(has_left)
    def _():
        copy(src_ref, own, 1, left).start()

    @pl.when(has_right)
    def _():
        copy(src_ref, own, 2, right).start()

    for d in range(1, nz):
        @pl.when(zl - d >= 0)
        def _():
            s = (zl - d) * 2 + c
            copy(out_ref.at[s], s, 0, partner).wait_recv()
            copy(out_ref.at[s], s, 0, partner).start()

            @pl.when(has_right)
            def _():
                copy(out_ref.at[s], s, 2, right).start()

        @pl.when(zl + d <= nz - 1)
        def _():
            s = (zl + d) * 2 + c
            copy(out_ref.at[s], s, 0, partner).wait_recv()
            copy(out_ref.at[s], s, 0, partner).start()

            @pl.when(has_left)
            def _():
                copy(out_ref.at[s], s, 1, left).start()

    for z in range(nz):
        s = z * 2 + (1 - c)
        copy(out_ref.at[s], s, 0, partner).wait_recv()

    mine.wait()
    for z in range(nz):
        s = z * 2 + c
        copy(out_ref.at[s], s, 0, partner).wait_send()

        @pl.when(has_left & (z >= zl))
        def _():
            copy(out_ref.at[s], s, 1, left).wait_send()

        @pl.when(has_right & (z <= zl))
        def _():
            copy(out_ref.at[s], s, 2, right).wait_send()


def row_gather(placed, nz):
    groups = 2 * nz
    return pl.pallas_call(
        functools.partial(gather_kernel, nz),
        out_shape=jax.ShapeDtypeStruct((groups,) + placed.shape, placed.dtype),
        in_specs=[pl.BlockSpec(memory_space=pltpu.VMEM)],
        out_specs=pl.BlockSpec(memory_space=pl.ANY),
        scratch_shapes=[
            pltpu.SemaphoreType.DMA(()),
            pltpu.SemaphoreType.DMA((groups, 3)),
            pltpu.SemaphoreType.DMA((groups,)),
        ],
        compiler_params=pltpu.CompilerParams(collective_id=0, has_side_effects=True),
    )(placed)


def local(residual_in, amplitudes, integral_tiles, tile_reader, tile_k, tile_column):
    targets = lax.axis_size("bulk")
    height, width = integral_tiles.shape[1], integral_tiles.shape[2]
    filled, local_index, slot_position = bucket_slots(
        tile_reader, tile_k, tile_column, targets, SLOT
    )
    picked = jnp.take(integral_tiles, local_index.reshape(-1), axis=0)
    picked = jnp.where(filled.reshape(-1)[:, None, None] > 0, picked, 0.0)
    outgoing = picked.reshape(targets, SLOT, height, width)
    arrived = lax.all_to_all(outgoing, "bulk", split_axis=0, concat_axis=0, tiled=True)
    position = lax.all_to_all(slot_position, "bulk", split_axis=0, concat_axis=0, tiled=True)
    arrived = arrived.reshape(targets * SLOT, height * width)
    position = position.reshape(-1)
    table = (position[None, :] == jnp.arange(KT * CT, dtype=jnp.int32)[:, None]).astype(jnp.float32)
    placed = jnp.dot(table, arrived, precision=lax.Precision.HIGHEST)
    placed = placed.reshape(KT, CT, height, width).transpose(0, 2, 1, 3).reshape(KT * height, CT * width)
    nz = lax.axis_size("zl")
    gathered = row_gather(placed, nz)
    dense = gathered.reshape(-1, CT * width)
    amps = lax.all_gather(amplitudes, "bulk", axis=1, tiled=True)
    rows = amps.shape[0]
    groups = gathered.shape[0]
    amps = amps.reshape(rows, KT, groups, height).transpose(0, 2, 1, 3).reshape(rows, -1)
    return residual_in + jnp.dot(amps, dense, precision=lax.Precision.HIGHEST)


def solution(mesh):
    row_size = mesh.shape["row"]
    devices = np.asarray(mesh.devices).reshape(row_size // 2, 2, mesh.shape["bulk"])
    inner = Mesh(devices, ("zl", "core", "bulk"))
    row = ("zl", "core")
    placed = (
        P(row, "bulk"),
        P(row, "bulk"),
        P("bulk", row, None),
        P("bulk", None),
        P("bulk"),
        P("bulk"),
    )
    return jax.shard_map(
        local, mesh=inner, in_specs=placed, out_specs=P(row, "bulk"), check_vma=False
    )
```

time: 377 us -> 207 us (0.55)
  waiting for transfers between devices: 297 us -> 40 us
  Pallas kernels: 0 us -> 93.7 us
  starting transfers between devices: 31.5 us -> 25.2 us
    all_gather x1, waiting for transfers between devices: 142 us -> 0.02 us  [local(): amps = lax.all_gather(amplitudes, 'bulk', axis=1, tiled=True)]
    all_gather x2 -> x0, waiting for transfers between devices: 102 us -> none  [the longest x1 80 us: local(): gathered = lax.all_gather(placed, 'zl', axis=0, tiled=False)]
    pallas_call x0 -> x1, Pallas kernels: none -> 93.7 us  [row_gather(): pl.pallas_call(functools.partial(gather_kernel, nz), out_shape=jax.ShapeD...]
    all_to_all x2 -> x1, waiting for transfers between devices: 22.4 us -> 10.3 us  [local(): lax.all_to_all(slot_position, 'bulk', split_axis=0, concat_axis=0, tiled=...]
    all_to_all x2 -> x1, starting transfers between devices: 25.1 us -> 19.1 us  [local(): lax.all_to_all(slot_position, 'bulk', split_axis=0, concat_axis=0, tiled=...]
  transfers between devices with their start and end apart: 6 -> 3, of which waited for: 6 -> 2; matrix products, arithmetic and copies ran while one was open for 2% -> 7% of each run, Pallas kernels for 0% -> 46%
where the time goes in v2:
time: 207 us; the launch traced here: 205 us
  Pallas kernels  93.7 us (45%)
  waiting for transfers between devices  40 us (19%)
  starting transfers between devices  25.2 us (12%)
  matrix products  16.2 us (8%)
  between operations  13.5 us (7%)
  local copies, waits for them, and re-layouts  11.4 us (6%)
  other arithmetic  4.72 us (2%)
    pallas_call x1, Pallas kernels, row_gather(): pl.pallas_call(functools.partial(gather_kernel, nz), out_shape=jax.ShapeD...  93.7 us
    all_to_all x1, waiting for transfers between devices, local(): lax.all_to_all(outgoing, 'bulk', split_axis=0, concat_axis=0, tiled=True)  29 us
    all_to_all x1, starting transfers between devices, local(): lax.all_to_all(slot_position, 'bulk', split_axis=0, concat_axis=0, tiled=...  19.1 us
    dot_general x1, matrix products, local(): return residual_in + jnp.dot(amps, dense, precision=lax.Precision.HIGHEST)  15.5 us
    all_to_all x1, waiting for transfers between devices, local(): lax.all_to_all(slot_position, 'bulk', split_axis=0, concat_axis=0, tiled=...  10.3 us
    all_to_all x1, starting transfers between devices, local(): lax.all_to_all(outgoing, 'bulk', split_axis=0, concat_axis=0, tiled=True)  6.13 us
  transfers between devices with their start and end apart: 3, of which 2 were waited for; matrix products, arithmetic and copies ran while one was open for 7% of the time, Pallas kernels for 46%

profile of v2, /device:TPU:6, one launch (start us, length us, event | category | flops | bytes accessed | tf_op | source)
XLA Modules:
  0.0 204.8 jit_solution(9864033381554661118)
XLA Ops:
  6.5 0.0 copy-start
  6.5 0.0 all-gather.2.cloned.1.call-start
  6.5 0.7 all-gather.2.cloned.1.call-update
  7.3 0.8 fusion.9
  8.1 0.1 reduce_window_sum.11
  8.2 0.8 select_reduce_fusion
  9.0 0.7 multiply_add_fusion.1
  9.7 0.2 fusion.1
  9.9 0.7 copy.29
  10.6 19.1 %all-to-all-start = ((s32[64,1,2]{2,1,0:T(1,128)}), s32[64,1,2]{2,1,0:T(1,128)S(1)}, u32[]{:S(2)}, u32[]{:S(2)}) async-start(s32[64,1,2]{2,1,0:T(1,128)} %copy.29), calls=%async_computation | async-start | bytes 65536 | tf_op jit(solution)/shard_map/all_to_all | solution.py:144
  29.7 0.1 copy.32
  29.8 0.1 copy.31
  29.9 0.1 copy.30
  30.0 0.1 reshape.152
  30.2 0.0 copy-done
  30.2 0.8 gather_fusion
  31.0 1.3 select_select_fusion
  32.3 10.3 %all-to-all-done = s32[64,1,2]{2,1,0:T(1,128)S(1)} async-done(((s32[64,1,2]{2,1,0:T(1,128)}), s32[64,1,2]{2,1,0:T(1,128)S(1)}, u32[]{:S(2)}, u32[]{:S(2)}) %all-to-all-start) | async-done | bytes 544 | tf_op jit(solution)/shard_map/all_to_all | solution.py:144
  42.6 6.1 %all-to-all-start.1 = ((f32[64,2,16,128]{3,2,1,0:T(8,128)}), f32[64,2,16,128]{3,2,1,0:T(8,128)S(1)}, u32[]{:S(2)}, u32[]{:S(2)}) async-start(f32[64,2,16,128]{3,2,1,0:T(8,128)} %select_select_fusion), calls=%async_computation.1 | async-start | bytes 2097152 | tf_op jit(solution)/shard_map/all_to_all | solution.py:143
  48.7 1.6 copy.35
  50.3 0.6 broadcast.110
  50.9 0.8 reduce.3
  51.7 0.1 eq.80
  51.8 29.0 %all-to-all-done.1 = f32[64,2,16,128]{3,2,1,0:T(8,128)S(1)} async-done(((f32[64,2,16,128]{3,2,1,0:T(8,128)}), f32[64,2,16,128]{3,2,1,0:T(8,128)S(1)}, u32[]{:S(2)}, u32[]{:S(2)}) %all-to-all-start.1) | async-done | bytes 1048608 | tf_op jit(solution)/shard_map/all_to_all | solution.py:143
  80.8 1.3 copy.43
  82.1 1.5 copy.33
  83.6 0.7 fusion.3
  84.4 1.2 copy.42
  85.5 93.7 %shard_map.64 = f32[8,256,1024]{2,1,0:T(8,128)} custom-call(f32[256,1024]{1,0:T(8,128)} %bitcast.42), custom_call_target="tpu_custom_call" | custom-call | tf_op jit(solution)/shard_map/pallas_call | solution.py:120
  179.2 0.0 all-gather.2.cloned.1.call-done
  179.2 1.8 copy.34
  181.1 15.5 %fusion = f32[256,1024]{0,1:T(8,128)S(1)} fusion(f32[256,1024]{0,1:T(8,128)S(1)} %copy.35, f32[2048,1024]{1,0:T(8,128)} %bitcast.40, f32[256,2048]{0,1:T(8,128)S(1)} %bitcast.41), kind=kOutput, calls=%fused_computation.2 | convolution fusion | flops 6442713088 | bytes 12582912 | tf_op jit(solution)/shard_map/dot_general | solution.py:157
  196.6 1.3 copy.36
  (6 shorter events, 0.0 us)
Async XLA Ops:
  6.5 23.7 %copy-start = (f32[64,16,128]{2,1,0:T(8,128)S(1)}, f32[64,16,128]{2,1,0:T(8,128)}, u32[]{:S(2)}) copy-start(f32[64,16,128]{2,1,0:T(8,128)} %param.8) | copy-start | bytes 1572868
  6.5 172.7 %all-gather.2.cloned.1.call-start = ((), (), s32[]{:S(2)}) async-start(), calls=%async_computation.2 | async-start | bytes 2129920 | tf_op jit(solution)/shard_map/all_gather | solution.py:153
  10.6 32.0 %all-to-all-start = ((s32[64,1,2]{2,1,0:T(1,128)}), s32[64,1,2]{2,1,0:T(1,128)S(1)}, u32[]{:S(2)}, u32[]{:S(2)}) async-start(s32[64,1,2]{2,1,0:T(1,128)} %copy.29), calls=%async_computation | async-start | bytes 65536 | tf_op jit(solution)/shard_map/all_to_all | solution.py:144
  42.6 38.2 %all-to-all-start.1 = ((f32[64,2,16,128]{3,2,1,0:T(8,128)}), f32[64,2,16,128]{3,2,1,0:T(8,128)S(1)}, u32[]{:S(2)}, u32[]{:S(2)}) async-start(f32[64,2,16,128]{3,2,1,0:T(8,128)} %select_select_fusion), calls=%async_computation.1 | async-start | bytes 2097152 | tf_op jit(solution)/shard_map/all_to_all | solution.py:143
Sparse Core Ops, SparseCore 0:
  11.9 137.5 all-gather.1

commit v3 on v2

--- a/solution.py
+++ b/solution.py
@@ -139,11 +139,13 @@
     )
     picked = jnp.take(integral_tiles, local_index.reshape(-1), axis=0)
     picked = jnp.where(filled.reshape(-1)[:, None, None] > 0, picked, 0.0)
-    outgoing = picked.reshape(targets, SLOT, height, width)
+    label = jnp.zeros((targets, 1, width), jnp.float32).at[:, 0, :SLOT].set(
+        slot_position.reshape(targets, SLOT).astype(jnp.float32)
+    )
+    outgoing = jnp.concatenate([picked.reshape(targets, SLOT * height, width), label], axis=1)
     arrived = lax.all_to_all(outgoing, "bulk", split_axis=0, concat_axis=0, tiled=True)
-    position = lax.all_to_all(slot_position, "bulk", split_axis=0, concat_axis=0, tiled=True)
-    arrived = arrived.reshape(targets * SLOT, height * width)
-    position = position.reshape(-1)
+    position = arrived[:, SLOT * height, :SLOT].reshape(-1).astype(jnp.int32)
+    arrived = arrived[:, : SLOT * height, :].reshape(targets * SLOT, height * width)
     table = (position[None, :] == jnp.arange(KT * CT, dtype=jnp.int32)[:, None]).astype(jnp.float32)
     placed = jnp.dot(table, arrived, precision=lax.Precision.HIGHEST)
     placed = placed.reshape(KT, CT, height, width).transpose(0, 2, 1, 3).reshape(KT * height, CT * width)

time: 207 us -> 207 us (level)
  the two profiles are of different devices: /device:TPU:6 before, /device:TPU:66 now
where the time goes in v3:
time: 207 us
  Pallas kernels  92 us (44%)
  waiting for transfers between devices  49.7 us (24%)
  starting transfers between devices  18.2 us (9%)
  matrix products  16.2 us (8%)
  between operations  13.5 us (7%)
  local copies, waits for them, and re-layouts  12.3 us (6%)
  other arithmetic  4.61 us (2%)
    pallas_call x1, Pallas kernels, row_gather(): pl.pallas_call(functools.partial(gather_kernel, nz), out_shape=jax.ShapeD...  92 us
    all_to_all x1, waiting for transfers between devices, local(): lax.all_to_all(outgoing, 'bulk', split_axis=0, concat_axis=0, tiled=True)  36.3 us
    all_to_all x1, starting transfers between devices, local(): lax.all_to_all(outgoing, 'bulk', split_axis=0, concat_axis=0, tiled=True)  18.2 us
    dot_general x1, matrix products, local(): return residual_in + jnp.dot(amps, dense, precision=lax.Precision.HIGHEST)  15.5 us
    all_gather x1, waiting for transfers between devices, local(): amps = lax.all_gather(amplitudes, 'bulk', axis=1, tiled=True)  12.6 us
  transfers between devices with their start and end apart: 2, of which 2 were waited for; matrix products, arithmetic and copies ran while one was open for 7% of the time, Pallas kernels for 45%

profile of v3, /device:TPU:66, one launch (start us, length us, event | category | flops | bytes accessed | tf_op | source)
XLA Modules:
  0.0 206.5 jit_solution(5765082737307281035)
XLA Ops:
  6.5 0.0 copy-start
  6.5 0.0 all-gather.2.cloned.1.call-start
  6.5 0.7 all-gather.2.cloned.1.call-update
  7.3 0.8 fusion.11
  8.1 0.1 reduce_window_sum.11
  8.2 0.8 select_reduce_fusion
  9.0 0.7 multiply_add_fusion.1
  9.7 0.2 fusion.2
  9.9 0.1 copy.29
  10.0 0.1 copy.28
  10.1 0.1 copy.27
  10.2 0.1 reshape.193
  10.4 0.1 copy.36
  10.5 0.0 copy-done
  10.5 0.8 gather_fusion
  11.3 0.7 fusion.1
  12.0 1.2 select_maximum_fusion
  13.1 18.2 %all-to-all-start = ((f32[64,33,128]{2,1,0:T(8,128)}), f32[64,33,128]{2,1,0:T(8,128)S(1)}, u32[]{:S(2)}, u32[]{:S(2)}) async-start(f32[64,33,128]{2,1,0:T(8,128)} %select_maximum_fusion), calls=%async_computation | async-start | bytes 2621440 | tf_op jit(solution)/shard_map/all_to_all | solution.py:146
  31.3 1.6 copy.33
  32.9 36.3 %all-to-all-done = f32[64,33,128]{2,1,0:T(8,128)S(1)} async-done(((f32[64,33,128]{2,1,0:T(8,128)}), f32[64,33,128]{2,1,0:T(8,128)S(1)}, u32[]{:S(2)}, u32[]{:S(2)}) %all-to-all-start) | async-done | bytes 1081376 | tf_op jit(solution)/shard_map/all_to_all | solution.py:146
  69.3 0.1 fusion.7
  69.4 0.1 convert_element_type.46
  69.5 1.1 slice.34
  70.6 2.4 %reshape.194 = f32[128,2048]{1,0:T(8,128)} reshape(f32[64,32,128]{2,1,0:T(8,128)} %slice.34) | data formatting | bytes 2097152 | tf_op jit(solution)/shard_map/reshape | solution.py:148
  73.0 1.5 copy.31
  74.5 0.7 fusion.4
  75.2 1.2 copy.39
  76.4 92.0 %shard_map.64 = f32[8,256,1024]{2,1,0:T(8,128)} custom-call(f32[256,1024]{1,0:T(8,128)} %bitcast.41), custom_call_target="tpu_custom_call" | custom-call | tf_op jit(solution)/shard_map/pallas_call | solution.py:120
  168.4 12.6 %all-gather.2.cloned.1.call-done = f32[256,2048]{0,1:T(8,128)} async-done(((f32[256,32]{0,1:T(8,128)}), f32[256,2048]{0,1:T(8,128)}) %all-gather.2.cloned.1.call-update) | async-done | bytes 2097168 | tf_op jit(solution)/shard_map/all_gather | solution.py:155
  181.0 1.8 copy.32
  182.8 15.5 %fusion = f32[256,1024]{0,1:T(8,128)S(1)} fusion(f32[256,1024]{0,1:T(8,128)S(1)} %copy.33, f32[2048,1024]{1,0:T(8,128)} %bitcast.39, f32[256,2048]{0,1:T(8,128)S(1)} %bitcast.40), kind=kOutput, calls=%fused_computation.4 | convolution fusion | flops 6442713088 | bytes 12582912 | tf_op jit(solution)/shard_map/dot_general | solution.py:159
  198.4 1.3 copy.34
  (8 shorter events, 0.1 us)
Async XLA Ops:
  6.5 3.9 %copy-start = (f32[64,16,128]{2,1,0:T(8,128)S(1)}, f32[64,16,128]{2,1,0:T(8,128)}, u32[]{:S(2)}) copy-start(f32[64,16,128]{2,1,0:T(8,128)} %param.10) | copy-start | bytes 1572868
  6.5 174.5 %all-gather.2.cloned.1.call-start = ((), (), s32[]{:S(2)}) async-start(), calls=%async_computation.1 | async-start | bytes 2129920 | tf_op jit(solution)/shard_map/all_gather | solution.py:155
  13.1 56.1 %all-to-all-start = ((f32[64,33,128]{2,1,0:T(8,128)}), f32[64,33,128]{2,1,0:T(8,128)S(1)}, u32[]{:S(2)}, u32[]{:S(2)}) async-start(f32[64,33,128]{2,1,0:T(8,128)} %select_maximum_fusion), calls=%async_computation | async-start | bytes 2621440 | tf_op jit(solution)/shard_map/all_to_all | solution.py:146
Sparse Core Ops, SparseCore 0:
  11.9 169.0 all-gather.1

commit v4 on v3

--- a/solution.py
+++ b/solution.py
@@ -131,6 +131,76 @@
     )(placed)
 
 
+def exchange_kernel(nb, src_ref, out_ref, local_sem, send_sem, recv_sem):
+    zl = lax.axis_index("zl")
+    c = lax.axis_index("core")
+    me = lax.axis_index("bulk")
+
+    barrier = pltpu.get_barrier_semaphore()
+
+    def greet(p, carry):
+        pl.semaphore_signal(barrier, 1, device_id=(zl, c, lax.rem(me + p, nb)), device_id_type=MESH)
+        return carry
+
+    lax.fori_loop(1, nb, greet, 0)
+    pl.semaphore_wait(barrier, nb - 1)
+
+    mine = pltpu.make_async_copy(src_ref.at[me], out_ref.at[me], local_sem)
+    mine.start()
+
+    def copy(p, dest):
+        return pltpu.make_async_remote_copy(
+            src_ref=src_ref.at[dest],
+            dst_ref=out_ref.at[me],
+            send_sem=send_sem.at[p],
+            recv_sem=recv_sem.at[me],
+            device_id=(zl, c, dest),
+            device_id_type=MESH,
+        )
+
+    def send(p, carry):
+        copy(p, lax.rem(me + p, nb)).start()
+        return carry
+
+    lax.fori_loop(1, nb, send, 0)
+
+    def receive(p, carry):
+        source = lax.rem(me + nb - p, nb)
+        pltpu.make_async_remote_copy(
+            src_ref=src_ref.at[source],
+            dst_ref=out_ref.at[source],
+            send_sem=send_sem.at[p],
+            recv_sem=recv_sem.at[source],
+            device_id=(zl, c, source),
+            device_id_type=MESH,
+        ).wait_recv()
+        return carry
+
+    lax.fori_loop(1, nb, receive, 0)
+    mine.wait()
+
+    def sent(p, carry):
+        copy(p, lax.rem(me + p, nb)).wait_send()
+        return carry
+
+    lax.fori_loop(1, nb, sent, 0)
+
+
+def bulk_exchange(outgoing, nb):
+    return pl.pallas_call(
+        functools.partial(exchange_kernel, nb),
+        out_shape=jax.ShapeDtypeStruct(outgoing.shape, outgoing.dtype),
+        in_specs=[pl.BlockSpec(memory_space=pltpu.VMEM)],
+        out_specs=pl.BlockSpec(memory_space=pltpu.VMEM),
+        scratch_shapes=[
+            pltpu.SemaphoreType.DMA(()),
+            pltpu.SemaphoreType.DMA((nb,)),
+            pltpu.SemaphoreType.DMA((nb,)),
+        ],
+        compiler_params=pltpu.CompilerParams(collective_id=1, has_side_effects=True),
+    )(outgoing)
+
+
 def local(residual_in, amplitudes, integral_tiles, tile_reader, tile_k, tile_column):
     targets = lax.axis_size("bulk")
     height, width = integral_tiles.shape[1], integral_tiles.shape[2]
@@ -143,7 +213,7 @@
         slot_position.reshape(targets, SLOT).astype(jnp.float32)
     )
     outgoing = jnp.concatenate([picked.reshape(targets, SLOT * height, width), label], axis=1)
-    arrived = lax.all_to_all(outgoing, "bulk", split_axis=0, concat_axis=0, tiled=True)
+    arrived = bulk_exchange(outgoing, targets)
     position = arrived[:, SLOT * height, :SLOT].reshape(-1).astype(jnp.int32)
     arrived = arrived[:, : SLOT * height, :].reshape(targets * SLOT, height * width)
     table = (position[None, :] == jnp.arange(KT * CT, dtype=jnp.int32)[:, None]).astype(jnp.float32)

time: 207 us -> 208 us (level)
  Pallas kernels: 92 us -> 149 us
  waiting for transfers between devices: 49.7 us -> 15.6 us
  starting transfers between devices: 18.2 us -> 0.01 us
  local copies, waits for them, and re-layouts: 12.3 us -> 8.15 us
    pallas_call x0 -> x1, Pallas kernels: none -> 52.3 us  [bulk_exchange(): pl.pallas_call(functools.partial(exchange_kernel, nb), out_shape=jax.Shap...]
    all_to_all x1 -> x0, waiting for transfers between devices: 36.3 us -> none  [local(): lax.all_to_all(outgoing, 'bulk', split_axis=0, concat_axis=0, tiled=True)]
    all_to_all x1 -> x0, starting transfers between devices: 18.2 us -> none  [local(): lax.all_to_all(outgoing, 'bulk', split_axis=0, concat_axis=0, tiled=True)]
    pallas_call x1, Pallas kernels: 92 us -> 96.5 us  [row_gather(): pl.pallas_call(functools.partial(gather_kernel, nz), out_shape=jax.ShapeD...]
    all_gather x1, waiting for transfers between devices: 12.6 us -> 14.9 us  [local(): amps = lax.all_gather(amplitudes, 'bulk', axis=1, tiled=True)]
    reshape x1, local copies, waits for them, and re-layouts: 2.37 us -> 0.16 us  [local(): arrived[:, :SLOT * height, :].reshape(targets * SLOT, height * width)]
  transfers between devices with their start and end apart: 2 -> 1, of which waited for: 2 -> 1; matrix products, arithmetic and copies ran while one was open for 7% -> 5% of each run, Pallas kernels for 45% -> 72%
where the time goes in v4:
time: 208 us
  Pallas kernels  149 us (72%)
  matrix products  16.2 us (8%)
  waiting for transfers between devices  15.6 us (8%)
  between operations  13.5 us (6%)
  local copies, waits for them, and re-layouts  8.15 us (4%)
  other arithmetic  5.56 us (3%)
    pallas_call x1, Pallas kernels, row_gather(): pl.pallas_call(functools.partial(gather_kernel, nz), out_shape=jax.ShapeD...  96.5 us
    pallas_call x1, Pallas kernels, bulk_exchange(): pl.pallas_call(functools.partial(exchange_kernel, nb), out_shape=jax.Shap...  52.3 us
    dot_general x1, matrix products, local(): return residual_in + jnp.dot(amps, dense, precision=lax.Precision.HIGHEST)  15.5 us
    all_gather x1, waiting for transfers between devices, local(): amps = lax.all_gather(amplitudes, 'bulk', axis=1, tiled=True)  14.9 us
  transfers between devices with their start and end apart: 1, of which 1 were waited for; matrix products, arithmetic and copies ran while one was open for 5% of the time, Pallas kernels for 72%

profile of v4, /device:TPU:66, one launch (start us, length us, event | category | flops | bytes accessed | tf_op | source)
XLA Modules:
  0.0 207.9 jit_solution(8920174725749455525)
XLA Ops:
  6.5 0.0 copy-start
  6.5 0.0 all-gather.2.cloned.1.call-start
  6.5 0.7 all-gather.2.cloned.1.call-update
  7.3 0.8 fusion.10
  8.1 0.1 reduce_window_sum.11
  8.2 0.8 select_reduce_fusion
  9.0 0.7 multiply_add_fusion.1
  9.7 0.2 fusion.2
  9.9 0.1 copy.31
  10.0 0.1 copy.30
  10.1 0.1 copy.29
  10.2 0.1 reshape.193
  10.4 0.1 copy.32
  10.5 0.0 copy-done
  10.5 0.8 gather_fusion
  11.3 0.7 fusion.1
  12.0 1.2 select_maximum_fusion.src_ref
  13.1 52.3 %shard_map.64 = f32[64,33,128]{2,1,0:T(8,128)} custom-call(f32[64,33,128]{2,1,0:T(8,128)} %select_maximum_fusion.src_ref), custom_call_target="tpu_custom_call" | custom-call | tf_op jit(solution)/shard_map/pallas_call | solution.py:190
  65.5 1.3 slice.30
  66.8 1.1 convert_reduce_fusion
  67.8 0.1 convert_element_type.46
  68.0 0.2 reshape.194
  68.1 0.3 copy.33
  68.5 0.7 fusion.4
  69.2 0.0 copy-start.1
  69.2 1.2 copy.40
  70.4 0.3 copy-done.1
  70.6 0.3 copy.35
  71.0 96.5 %shard_map.65 = f32[8,256,1024]{2,1,0:T(8,128)} custom-call(f32[256,1024]{1,0:T(8,128)} %bitcast.41), custom_call_target="tpu_custom_call" | custom-call | tf_op jit(solution)/shard_map/pallas_call | solution.py:120
  167.5 14.9 %all-gather.2.cloned.1.call-done = f32[256,2048]{0,1:T(8,128)} async-done(((f32[256,32]{0,1:T(8,128)}), f32[256,2048]{0,1:T(8,128)}) %all-gather.2.cloned.1.call-update) | async-done | bytes 2097168 | tf_op jit(solution)/shard_map/all_gather | solution.py:225
  182.4 1.8 copy.34
  184.2 15.5 %fusion = f32[256,1024]{0,1:T(8,128)S(1)} fusion(f32[256,1024]{0,1:T(8,128)S(1)} %copy.35, f32[2048,1024]{1,0:T(8,128)} %bitcast.39, f32[256,2048]{0,1:T(8,128)S(1)} %bitcast.40), kind=kOutput, calls=%fused_computation.4 | convolution fusion | flops 6442713088 | bytes 12582912 | tf_op jit(solution)/shard_map/dot_general | solution.py:229
  199.8 1.3 copy.36
  (8 shorter events, 0.1 us)
Async XLA Ops:
  6.5 3.9 %copy-start = (f32[64,16,128]{2,1,0:T(8,128)S(1)}, f32[64,16,128]{2,1,0:T(8,128)}, u32[]{:S(2)}) copy-start(f32[64,16,128]{2,1,0:T(8,128)} %param.10) | copy-start | bytes 1572868
  6.5 175.8 %all-gather.2.cloned.1.call-start = ((), (), s32[]{:S(2)}) async-start(), calls=%async_computation | async-start | bytes 2129920 | tf_op jit(solution)/shard_map/all_gather | solution.py:225
  69.2 1.5 copy-start.1
Sparse Core Ops, SparseCore 0:
  11.9 170.4 all-gather.1

commit v5 on v4

--- a/solution.py
+++ b/solution.py
@@ -121,7 +121,7 @@
         functools.partial(gather_kernel, nz),
         out_shape=jax.ShapeDtypeStruct((groups,) + placed.shape, placed.dtype),
         in_specs=[pl.BlockSpec(memory_space=pltpu.VMEM)],
-        out_specs=pl.BlockSpec(memory_space=pl.ANY),
+        out_specs=pl.BlockSpec(memory_space=pltpu.VMEM),
         scratch_shapes=[
             pltpu.SemaphoreType.DMA(()),
             pltpu.SemaphoreType.DMA((groups, 3)),
@@ -226,7 +226,7 @@
     rows = amps.shape[0]
     groups = gathered.shape[0]
     amps = amps.reshape(rows, KT, groups, height).transpose(0, 2, 1, 3).reshape(rows, -1)
-    return residual_in + jnp.dot(amps, dense, precision=lax.Precision.HIGHEST)
+    return residual_in + jnp.dot(amps, dense, precision=lax.Precision.HIGH)
 
 
 def solution(mesh):

time: 208 us -> 202 us (0.971)
  matrix products: 16.2 us -> 10 us
  Pallas kernels: 149 us -> 152 us
  waiting for transfers between devices: 15.6 us -> 12.8 us
    dot_general x1, matrix products: 15.5 us -> 9.31 us  [local(): return residual_in + jnp.dot(amps, dense, precision=lax.Precision.HIGH)]
    all_gather x1, waiting for transfers between devices: 14.9 us -> 12.1 us  [local(): amps = lax.all_gather(amplitudes, 'bulk', axis=1, tiled=True)]
    pallas_call x1, Pallas kernels: 96.5 us -> 99.3 us  [row_gather(): pl.pallas_call(functools.partial(gather_kernel, nz), out_shape=jax.ShapeD...]
  transfers between devices with their start and end apart: 1 -> 1, of which waited for: 1 -> 1; matrix products, arithmetic and copies ran while one was open for 5% -> 5% of each run, Pallas kernels for 72% -> 75%
where the time goes in v5:
time: 202 us
  Pallas kernels  152 us (75%)
  between operations  13.5 us (7%)
  waiting for transfers between devices  12.8 us (6%)
  matrix products  10 us (5%)
  local copies, waits for them, and re-layouts  8.11 us (4%)
  other arithmetic  5.56 us (3%)
    pallas_call x1, Pallas kernels, row_gather(): pl.pallas_call(functools.partial(gather_kernel, nz), out_shape=jax.ShapeD...  99.3 us
    pallas_call x1, Pallas kernels, bulk_exchange(): pl.pallas_call(functools.partial(exchange_kernel, nb), out_shape=jax.Shap...  52.3 us
    all_gather x1, waiting for transfers between devices, local(): amps = lax.all_gather(amplitudes, 'bulk', axis=1, tiled=True)  12.1 us
    dot_general x1, matrix products, local(): return residual_in + jnp.dot(amps, dense, precision=lax.Precision.HIGH)  9.31 us
  transfers between devices with their start and end apart: 1, of which 1 were waited for; matrix products, arithmetic and copies ran while one was open for 5% of the time, Pallas kernels for 75%

profile of v5, /device:TPU:66, one launch (start us, length us, event | category | flops | bytes accessed | tf_op | source)
XLA Modules:
  0.0 201.6 jit_solution(14019368247642384579)
XLA Ops:
  6.5 0.0 copy-start
  6.5 0.0 all-gather.2.cloned.1.call-start
  6.5 0.7 all-gather.2.cloned.1.call-update
  7.3 0.8 fusion.10
  8.1 0.1 reduce_window_sum.11
  8.2 0.8 select_reduce_fusion
  9.0 0.7 multiply_add_fusion.1
  9.7 0.2 fusion.2
  9.9 0.1 copy.31
  10.0 0.1 copy.30
  10.1 0.1 copy.29
  10.2 0.1 reshape.193
  10.4 0.1 copy.32
  10.5 0.0 copy-done
  10.5 0.8 gather_fusion
  11.3 0.7 fusion.1
  12.0 1.2 select_maximum_fusion.src_ref
  13.1 52.3 %shard_map.64 = f32[64,33,128]{2,1,0:T(8,128)} custom-call(f32[64,33,128]{2,1,0:T(8,128)} %select_maximum_fusion.src_ref), custom_call_target="tpu_custom_call" | custom-call | tf_op jit(solution)/shard_map/pallas_call | solution.py:190
  65.5 1.3 slice.30
  66.8 1.1 convert_reduce_fusion
  67.8 0.1 convert_element_type.46
  68.0 0.2 reshape.194
  68.1 0.3 copy.33
  68.5 0.7 fusion.4
  69.2 0.0 copy-start.1
  69.2 1.2 copy.40
  70.4 0.3 copy-done.1
  70.6 0.3 copy.35
  71.0 99.3 %shard_map.65 = f32[8,256,1024]{2,1,0:T(8,128)} custom-call(f32[256,1024]{1,0:T(8,128)} %bitcast.41), custom_call_target="tpu_custom_call" | custom-call | tf_op jit(solution)/shard_map/pallas_call | solution.py:120
  170.3 12.1 %all-gather.2.cloned.1.call-done = f32[256,2048]{0,1:T(8,128)} async-done(((f32[256,32]{0,1:T(8,128)}), f32[256,2048]{0,1:T(8,128)}) %all-gather.2.cloned.1.call-update) | async-done | bytes 2097168 | tf_op jit(solution)/shard_map/all_gather | solution.py:225
  182.3 1.8 copy.34
  184.1 9.3 %fusion = f32[256,1024]{0,1:T(8,128)S(1)} fusion(f32[256,1024]{0,1:T(8,128)S(1)} %copy.35, f32[2048,1024]{1,0:T(8,128)} %bitcast.39, f32[256,2048]{0,1:T(8,128)S(1)} %bitcast.40), kind=kOutput, calls=%fused_computation.4 | convolution fusion | flops 3221487616 | bytes 12582912 | tf_op jit(solution)/shard_map/dot_general | solution.py:229
  193.5 1.3 copy.36
  (8 shorter events, 0.1 us)
Async XLA Ops:
  6.5 3.9 %copy-start = (f32[64,16,128]{2,1,0:T(8,128)S(1)}, f32[64,16,128]{2,1,0:T(8,128)}, u32[]{:S(2)}) copy-start(f32[64,16,128]{2,1,0:T(8,128)} %param.10) | copy-start | bytes 1572868
  6.5 175.8 %all-gather.2.cloned.1.call-start = ((), (), s32[]{:S(2)}) async-start(), calls=%async_computation | async-start | bytes 2129920 | tf_op jit(solution)/shard_map/all_gather | solution.py:225
  69.2 1.5 copy-start.1
Sparse Core Ops, SparseCore 0:
  11.9 170.4 all-gather.1

commit v6 on v5

--- a/solution.py
+++ b/solution.py
@@ -29,7 +29,7 @@
     return filled, local_index, slot_position
 
 
-def gather_kernel(nz, src_ref, out_ref, local_sem, send_sem, recv_sem):
+def gather_kernel(nz, src_ref, amps_ref, residual_ref, out_ref, held, send_sem, recv_sem):
     zl = lax.axis_index("zl")
     c = lax.axis_index("core")
     b = lax.axis_index("bulk")
@@ -57,15 +57,19 @@
     def copy(src, slot, kind, dev):
         return pltpu.make_async_remote_copy(
             src_ref=src,
-            dst_ref=out_ref.at[slot],
+            dst_ref=held.at[slot],
             send_sem=send_sem.at[slot, kind],
             recv_sem=recv_sem.at[slot],
             device_id=dev,
             device_id_type=MESH,
         )
 
-    mine = pltpu.make_async_copy(src_ref, out_ref.at[own], local_sem)
-    mine.start()
+    def accumulate(slot, block):
+        out_ref[...] += jnp.dot(
+            amps_ref[slot], block[...], precision=lax.Precision.HIGHEST,
+            preferred_element_type=jnp.float32,
+        )
+
     copy(src_ref, own, 0, partner).start()
 
     @pl.when(has_left)
@@ -75,60 +79,84 @@
     @pl.when(has_right)
     def _():
         copy(src_ref, own, 2, right).start()
+
+    out_ref[...] = residual_ref[...]
+    accumulate(own, src_ref)
 
     for d in range(1, nz):
         @pl.when(zl - d >= 0)
         def _():
             s = (zl - d) * 2 + c
-            copy(out_ref.at[s], s, 0, partner).wait_recv()
-            copy(out_ref.at[s], s, 0, partner).start()
+            copy(held.at[s], s, 0, partner).wait_recv()
+            copy(held.at[s], s, 0, partner).start()
 
             @pl.when(has_right)
             def _():
-                copy(out_ref.at[s], s, 2, right).start()
+                copy(held.at[s], s, 2, right).start()
+
+            accumulate(s, held.at[s])
 
         @pl.when(zl + d <= nz - 1)
         def _():
             s = (zl + d) * 2 + c
-            copy(out_ref.at[s], s, 0, partner).wait_recv()
-            copy(out_ref.at[s], s, 0, partner).start()
+            copy(held.at[s], s, 0, partner).wait_recv()
+            copy(held.at[s], s, 0, partner).start()
 
             @pl.when(has_left)
             def _():
-                copy(out_ref.at[s], s, 1, left).start()
+                copy(held.at[s], s, 1, left).start()
+
+            accumulate(s, held.at[s])
 
     for z in range(nz):
         s = z * 2 + (1 - c)
-        copy(out_ref.at[s], s, 0, partner).wait_recv()
-
-    mine.wait()
+        copy(held.at[s], s, 0, partner).wait_recv()
+        accumulate(s, held.at[s])
+
     for z in range(nz):
         s = z * 2 + c
-        copy(out_ref.at[s], s, 0, partner).wait_send()
-
-        @pl.when(has_left & (z >= zl))
-        def _():
-            copy(out_ref.at[s], s, 1, left).wait_send()
-
-        @pl.when(has_right & (z <= zl))
-        def _():
-            copy(out_ref.at[s], s, 2, right).wait_send()
-
-
-def row_gather(placed, nz):
+
+        @pl.when(z == zl)
+        def _():
+            copy(src_ref, s, 0, partner).wait_send()
+
+        @pl.when(z != zl)
+        def _():
+            copy(held.at[s], s, 0, partner).wait_send()
+
+        @pl.when(has_left & (z == zl))
+        def _():
+            copy(src_ref, s, 1, left).wait_send()
+
+        @pl.when(has_left & (z > zl))
+        def _():
+            copy(held.at[s], s, 1, left).wait_send()
+
+        @pl.when(has_right & (z == zl))
+        def _():
+            copy(src_ref, s, 2, right).wait_send()
+
+        @pl.when(has_right & (z < zl))
+        def _():
+            copy(held.at[s], s, 2, right).wait_send()
+
+
+def gather_contract(placed, amps3, residual, nz):
     groups = 2 * nz
     return pl.pallas_call(
         functools.partial(gather_kernel, nz),
-        out_shape=jax.ShapeDtypeStruct((groups,) + placed.shape, placed.dtype),
-        in_specs=[pl.BlockSpec(memory_space=pltpu.VMEM)],
+        out_shape=jax.ShapeDtypeStruct(residual.shape, jnp.float32),
+        in_specs=[pl.BlockSpec(memory_space=pltpu.VMEM)] * 3,
         out_specs=pl.BlockSpec(memory_space=pltpu.VMEM),
         scratch_shapes=[
-            pltpu.SemaphoreType.DMA(()),
+            pltpu.VMEM((groups,) + placed.shape, jnp.float32),
             pltpu.SemaphoreType.DMA((groups, 3)),
             pltpu.SemaphoreType.DMA((groups,)),
         ],
-        compiler_params=pltpu.CompilerParams(collective_id=0, has_side_effects=True),
-    )(placed)
+        compiler_params=pltpu.CompilerParams(
+            collective_id=0, has_side_effects=True, vmem_limit_bytes=48 * 1024 * 1024
+        ),
+    )(placed, amps3, residual)
 
 
 def exchange_kernel(nb, src_ref, out_ref, local_sem, send_sem, recv_sem):
@@ -209,24 +237,27 @@
     )
     picked = jnp.take(integral_tiles, local_index.reshape(-1), axis=0)
     picked = jnp.where(filled.reshape(-1)[:, None, None] > 0, picked, 0.0)
+    rows, own_cols = amplitudes.shape
     label = jnp.zeros((targets, 1, width), jnp.float32).at[:, 0, :SLOT].set(
         slot_position.reshape(targets, SLOT).astype(jnp.float32)
     )
-    outgoing = jnp.concatenate([picked.reshape(targets, SLOT * height, width), label], axis=1)
+    amp_rows = rows * own_cols // width
+    amp_block = jnp.broadcast_to(amplitudes.reshape(1, amp_rows, width), (targets, amp_rows, width))
+    outgoing = jnp.concatenate(
+        [picked.reshape(targets, SLOT * height, width), label, amp_block], axis=1
+    )
     arrived = bulk_exchange(outgoing, targets)
     position = arrived[:, SLOT * height, :SLOT].reshape(-1).astype(jnp.int32)
+    amps = arrived[:, SLOT * height + 1 :, :].reshape(targets, rows, own_cols)
+    amps = amps.transpose(1, 0, 2).reshape(rows, targets * own_cols)
     arrived = arrived[:, : SLOT * height, :].reshape(targets * SLOT, height * width)
     table = (position[None, :] == jnp.arange(KT * CT, dtype=jnp.int32)[:, None]).astype(jnp.float32)
     placed = jnp.dot(table, arrived, precision=lax.Precision.HIGHEST)
     placed = placed.reshape(KT, CT, height, width).transpose(0, 2, 1, 3).reshape(KT * height, CT * width)
     nz = lax.axis_size("zl")
-    gathered = row_gather(placed, nz)
-    dense = gathered.reshape(-1, CT * width)
-    amps = lax.all_gather(amplitudes, "bulk", axis=1, tiled=True)
-    rows = amps.shape[0]
-    groups = gathered.shape[0]
-    amps = amps.reshape(rows, KT, groups, height).transpose(0, 2, 1, 3).reshape(rows, -1)
-    return residual_in + jnp.dot(amps, dense, precision=lax.Precision.HIGH)
+    groups = 2 * nz
+    amps3 = amps.reshape(rows, KT, groups, height).transpose(2, 0, 1, 3).reshape(groups, rows, KT * height)
+    return gather_contract(placed, amps3, residual_in, nz)
 
 
 def solution(mesh):

time: 202 us -> 242 us (1.20)
  the two profiles are of different devices: /device:TPU:66 before, /device:TPU:6 now
where the time goes in v6:
time: 242 us; the launch traced here: 239 us
  Pallas kernels  205 us (85%)
  local copies, waits for them, and re-layouts  25.1 us (10%)
  other arithmetic  6.75 us (3%)
    pallas_call x1, Pallas kernels, bulk_exchange(): pl.pallas_call(functools.partial(exchange_kernel, nb), out_shape=jax.Shap...  121 us
    pallas_call x1, Pallas kernels, gather_contract(): pl.pallas_call(functools.partial(gather_kernel, nz), out_shape=jax.ShapeD...  84 us
    slice x2, local copies, waits for them, and re-layouts, local(): amps = arrived[:, SLOT * height + 1:, :].reshape(targets, rows, own_cols)  6.06 us
    unnamed x11, local copies, waits for them, and re-layouts  5.44 us

profile of v6, /device:TPU:6, one launch (start us, length us, event | category | flops | bytes accessed | tf_op | source)
XLA Modules:
  0.0 239.0 jit_solution(8427071316948879422)
XLA Ops:
  0.0 0.0 copy-start
  0.0 0.7 multiply_add_fusion.1
  0.7 0.8 fusion.11
  1.5 0.1 reduce_window_sum.11
  1.6 0.8 select_reduce_fusion
  2.5 0.2 fusion.3
  2.7 0.1 copy.23
  2.8 0.1 copy.22
  2.9 0.1 copy.24
  3.0 0.1 reshape.192
  3.2 0.1 copy.25
  3.3 0.9 copy.26
  4.2 0.1 broadcast_in_dim.54
  4.3 0.0 copy-done
  4.3 0.8 gather_fusion
  5.0 0.7 fusion.2
  5.8 0.2 broadcast_in_dim.55
  6.0 2.2 fusion.src_ref
  8.2 121.1 %shard_map.64 = f32[64,97,128]{2,1,0:T(8,128)} custom-call(f32[64,97,128]{2,1,0:T(8,128)} %fusion.src_ref), custom_call_target="tpu_custom_call" | custom-call | tf_op jit(solution)/shard_map/pallas_call | solution.py:218
  129.3 0.0 slice-start
  129.3 1.1 convert_reduce_fusion
  130.5 0.1 convert_element_type.46
  130.6 3.3 %slice.34 = f32[64,64,128]{2,1,0:T(8,128)} slice(f32[64,97,128]{2,1,0:T(8,128)} %shard_map.64), slice={[0:64], [33:97], [0:128]} | slice | bytes 4194304 | tf_op jit(solution)/shard_map/slice | solution.py:251
  134.0 0.0 slice-done
  134.0 1.1 reshape.193
  135.1 0.0 copy-start.3
  135.1 2.7 %copy.27 = f32[2048,128]{1,0:T(8,128)} copy(f32[2048,128]{0,1:T(8,128)} %bitcast.42) | data formatting | bytes 2097152 | tf_op jit(solution)/shard_map/dot_general | solution.py:255
  137.8 1.9 fusion.5
  139.7 1.2 copy.35
  140.9 0.0 copy-done.3
  140.9 2.7 %copy.28 = f32[64,64,128]{0,2,1:T(8,128)} copy(f32[64,64,128]{2,1,0:T(8,128)S(1)} %copy-done.3) | data formatting | bytes 4194304 | tf_op jit(solution)/shard_map/slice | solution.py:251
  143.6 4.5 %copy.29 = f32[256,64,32]{0,2,1:T(8,128)S(1)} copy(f32[256,64,32]{1,2,0:T(8,128)} %bitcast.36) | data formatting | bytes 4194304 | tf_op jit(solution)/shard_map/transpose | solution.py:252
  148.1 1.6 copy.30
  149.7 1.9 copy.31.amps_ref
  151.6 0.0 copy-start.1
  151.6 1.2 copy-done.1
  152.8 0.0 copy-start.2
  152.8 1.2 copy-done.2
  154.0 84.0 %shard_map.65 = f32[256,1024]{1,0:T(8,128)S(1)} custom-call(f32[256,1024]{1,0:T(8,128)S(1)} %bitcast.35, f32[8,256,256]{2,1,0:T(8,128)S(1)} %copy.31.amps_ref, f32[256,1024]{1,0:T(8,128)S(1)} %copy-done.2), custom_call_target="tpu_custom_call" | custom-call | tf_op jit(solution)/shard_map/pallas_call | solution.py:146
  238.1 1.0 copy.37
  (8 shorter events, 0.1 us)
Async XLA Ops:
  0.0 4.3 %copy-start = (f32[64,16,128]{2,1,0:T(8,128)S(1)}, f32[64,16,128]{2,1,0:T(8,128)}, u32[]{:S(2)}) copy-start(f32[64,16,128]{2,1,0:T(8,128)} %param.10) | copy-start | bytes 1572868
  129.3 4.6 %slice-start = ((f32[64,97,128]{2,1,0:T(8,128)}), f32[64,32,128]{2,1,0:T(8,128)S(1)}, s32[]{:S(2)}) async-start(f32[64,97,128]{2,1,0:T(8,128)} %shard_map.64), calls=%async_computation | async-start | bytes 2097152 | tf_op jit(solution)/shard_map/slice | solution.py:253
  135.1 5.8 %copy-start.3 = (f32[64,64,128]{2,1,0:T(8,128)S(1)}, f32[64,64,128]{2,1,0:T(8,128)}, u32[]{:S(2)}) copy-start(f32[64,64,128]{2,1,0:T(8,128)} %slice.34) | copy-start | bytes 6291460
  151.6 1.2 copy-start.1
  152.8 1.2 copy-start.2

commit v7 on v6

--- a/solution.py
+++ b/solution.py
@@ -29,16 +29,18 @@
     return filled, local_index, slot_position
 
 
-def gather_kernel(nz, src_ref, amps_ref, residual_ref, out_ref, held, send_sem, recv_sem):
+def contract_kernel(nz, nb, src_ref, mine_ref, residual_ref, out_ref, held, amps_buf,
+                    send_sem, recv_sem, amp_send, amp_recv):
     zl = lax.axis_index("zl")
     c = lax.axis_index("core")
-    b = lax.axis_index("bulk")
-    partner = (zl, 1 - c, b)
-    left = (zl - 1, c, b)
-    right = (zl + 1, c, b)
+    me = lax.axis_index("bulk")
+    partner = (zl, 1 - c, me)
+    left = (zl - 1, c, me)
+    right = (zl + 1, c, me)
     has_left = zl > 0
     has_right = zl < nz - 1
     own = zl * 2 + c
+    n_m = amps_buf.shape[0]
 
     barrier = pltpu.get_barrier_semaphore()
     pl.semaphore_signal(barrier, 1, device_id=partner, device_id_type=MESH)
@@ -51,8 +53,33 @@
     def _():
         pl.semaphore_signal(barrier, 1, device_id=right, device_id_type=MESH)
 
-    peers = 1 + has_left.astype(jnp.int32) + has_right.astype(jnp.int32)
+    def greet(p, carry):
+        pl.semaphore_signal(barrier, 1, device_id=(zl, c, lax.rem(me + p, nb)), device_id_type=MESH)
+        return carry
+
+    lax.fori_loop(1, nb, greet, 0)
+    peers = nb + has_left.astype(jnp.int32) + has_right.astype(jnp.int32)
     pl.semaphore_wait(barrier, peers)
+
+    my_m = lax.rem(me, n_m)
+    my_k = me // n_m
+
+    def amp_copy(p, dest):
+        return pltpu.make_async_remote_copy(
+            src_ref=mine_ref,
+            dst_ref=amps_buf.at[my_m, my_k],
+            send_sem=amp_send.at[p],
+            recv_sem=amp_recv.at[me],
+            device_id=(zl, c, dest),
+            device_id_type=MESH,
+        )
+
+    def amp_send_one(p, carry):
+        amp_copy(p, lax.rem(me + p, nb)).start()
+        return carry
+
+    lax.fori_loop(1, nb, amp_send_one, 0)
+    amps_buf[my_m, my_k] = mine_ref[...]
 
     def copy(src, slot, kind, dev):
         return pltpu.make_async_remote_copy(
@@ -64,12 +91,6 @@
             device_id_type=MESH,
         )
 
-    def accumulate(slot, block):
-        out_ref[...] += jnp.dot(
-            amps_ref[slot], block[...], precision=lax.Precision.HIGHEST,
-            preferred_element_type=jnp.float32,
-        )
-
     copy(src_ref, own, 0, partner).start()
 
     @pl.when(has_left)
@@ -80,8 +101,26 @@
     def _():
         copy(src_ref, own, 2, right).start()
 
-    out_ref[...] = residual_ref[...]
-    accumulate(own, src_ref)
+    def amp_wait(p, carry):
+        source = lax.rem(me + nb - p, nb)
+        pltpu.make_async_remote_copy(
+            src_ref=mine_ref,
+            dst_ref=amps_buf.at[lax.rem(source, n_m), source // n_m],
+            send_sem=amp_send.at[p],
+            recv_sem=amp_recv.at[source],
+            device_id=(zl, c, source),
+            device_id_type=MESH,
+        ).wait_recv()
+        return carry
+
+    def accumulate(slot, block):
+        half = held.shape[1] // amps_buf.shape[1]
+        part = amps_buf[slot // 2, :, pl.ds(lax.rem(slot, 2) * half, half), :]
+        lhs_t = part.reshape(-1, part.shape[-1])
+        out_ref[...] += jnp.dot(
+            lhs_t.T, block[...], precision=lax.Precision.HIGHEST,
+            preferred_element_type=jnp.float32,
+        )
 
     for d in range(1, nz):
         @pl.when(zl - d >= 0)
@@ -94,8 +133,6 @@
             def _():
                 copy(held.at[s], s, 2, right).start()
 
-            accumulate(s, held.at[s])
-
         @pl.when(zl + d <= nz - 1)
         def _():
             s = (zl + d) * 2 + c
@@ -106,6 +143,14 @@
             def _():
                 copy(held.at[s], s, 1, left).start()
 
+    lax.fori_loop(1, nb, amp_wait, 0)
+    out_ref[...] = residual_ref[...]
+    accumulate(own, src_ref)
+    for z in range(nz):
+        s = z * 2 + c
+
+        @pl.when(z != zl)
+        def _():
             accumulate(s, held.at[s])
 
     for z in range(nz):
@@ -140,23 +185,33 @@
         def _():
             copy(held.at[s], s, 2, right).wait_send()
 
-
-def gather_contract(placed, amps3, residual, nz):
+    def amp_sent(p, carry):
+        amp_copy(p, lax.rem(me + p, nb)).wait_send()
+        return carry
+
+    lax.fori_loop(1, nb, amp_sent, 0)
+
+
+def gather_contract(placed, mine_t, residual, nz, nb, n_m):
     groups = 2 * nz
+    n_k = nb // n_m
     return pl.pallas_call(
-        functools.partial(gather_kernel, nz),
+        functools.partial(contract_kernel, nz, nb),
         out_shape=jax.ShapeDtypeStruct(residual.shape, jnp.float32),
         in_specs=[pl.BlockSpec(memory_space=pltpu.VMEM)] * 3,
         out_specs=pl.BlockSpec(memory_space=pltpu.VMEM),
         scratch_shapes=[
             pltpu.VMEM((groups,) + placed.shape, jnp.float32),
+            pltpu.VMEM((n_m, n_k) + mine_t.shape, jnp.float32),
             pltpu.SemaphoreType.DMA((groups, 3)),
             pltpu.SemaphoreType.DMA((groups,)),
+            pltpu.SemaphoreType.DMA((nb,)),
+            pltpu.SemaphoreType.DMA((nb,)),
         ],
         compiler_params=pltpu.CompilerParams(
             collective_id=0, has_side_effects=True, vmem_limit_bytes=48 * 1024 * 1024
         ),
-    )(placed, amps3, residual)
+    )(placed, mine_t, residual)
 
 
 def exchange_kernel(nb, src_ref, out_ref, local_sem, send_sem, recv_sem):
@@ -237,27 +292,19 @@
     )
     picked = jnp.take(integral_tiles, local_index.reshape(-1), axis=0)
     picked = jnp.where(filled.reshape(-1)[:, None, None] > 0, picked, 0.0)
-    rows, own_cols = amplitudes.shape
     label = jnp.zeros((targets, 1, width), jnp.float32).at[:, 0, :SLOT].set(
         slot_position.reshape(targets, SLOT).astype(jnp.float32)
     )
-    amp_rows = rows * own_cols // width
-    amp_block = jnp.broadcast_to(amplitudes.reshape(1, amp_rows, width), (targets, amp_rows, width))
-    outgoing = jnp.concatenate(
-        [picked.reshape(targets, SLOT * height, width), label, amp_block], axis=1
-    )
+    outgoing = jnp.concatenate([picked.reshape(targets, SLOT * height, width), label], axis=1)
     arrived = bulk_exchange(outgoing, targets)
     position = arrived[:, SLOT * height, :SLOT].reshape(-1).astype(jnp.int32)
-    amps = arrived[:, SLOT * height + 1 :, :].reshape(targets, rows, own_cols)
-    amps = amps.transpose(1, 0, 2).reshape(rows, targets * own_cols)
     arrived = arrived[:, : SLOT * height, :].reshape(targets * SLOT, height * width)
     table = (position[None, :] == jnp.arange(KT * CT, dtype=jnp.int32)[:, None]).astype(jnp.float32)
     placed = jnp.dot(table, arrived, precision=lax.Precision.HIGHEST)
     placed = placed.reshape(KT, CT, height, width).transpose(0, 2, 1, 3).reshape(KT * height, CT * width)
     nz = lax.axis_size("zl")
-    groups = 2 * nz
-    amps3 = amps.reshape(rows, KT, groups, height).transpose(2, 0, 1, 3).reshape(groups, rows, KT * height)
-    return gather_contract(placed, amps3, residual_in, nz)
+    rows, own_cols = amplitudes.shape
+    return gather_contract(placed, amplitudes.T, residual_in, nz, targets, width // own_cols)
 
 
 def solution(mesh):

time: 242 us -> 207 us (0.86)
  local copies, waits for them, and re-layouts: 25.1 us -> 4.13 us
  Pallas kernels: 205 us -> 194 us
    pallas_call x1, Pallas kernels: 121 us -> 54.6 us  [bulk_exchange(): pl.pallas_call(functools.partial(exchange_kernel, nb), out_shape=jax.Shap...]
    pallas_call x1, Pallas kernels: 84 us -> 140 us  [gather_contract(): pl.pallas_call(functools.partial(contract_kernel, nz, nb), out_shape=jax....]
    transpose x2 -> x0, local copies, waits for them, and re-layouts: 6.06 us -> none  [the longest x1 4.47 us: local(): amps = amps.transpose(1, 0, 2).reshape(rows, targets * own_cols)]
    slice x2 -> x0, local copies, waits for them, and re-layouts: 6.06 us -> none  [local(): amps = arrived[:, SLOT * height + 1:, :].reshape(targets, rows, own_cols)]
    unnamed x11 -> x8, local copies, waits for them, and re-layouts: 5.44 us -> 2.18 us
where the time goes in v7:
time: 207 us; the launch traced here: 205 us
  Pallas kernels  194 us (94%)
  other arithmetic  5.71 us (3%)
  local copies, waits for them, and re-layouts  4.13 us (2%)
    pallas_call x1, Pallas kernels, gather_contract(): pl.pallas_call(functools.partial(contract_kernel, nz, nb), out_shape=jax....  140 us
    pallas_call x1, Pallas kernels, bulk_exchange(): pl.pallas_call(functools.partial(exchange_kernel, nb), out_shape=jax.Shap...  54.6 us

profile of v7, /device:TPU:6, one launch (start us, length us, event | category | flops | bytes accessed | tf_op | source)
XLA Modules:
  0.0 205.1 jit_solution(17803445760038190665)
XLA Ops:
  0.0 0.0 copy-start
  0.0 0.7 multiply_add_fusion.1
  0.7 0.8 fusion.9
  1.5 0.1 reduce_window_sum.11
  1.6 0.8 select_reduce_fusion
  2.5 0.2 fusion.1
  2.7 0.1 copy.18
  2.8 0.1 copy.17
  2.9 0.1 copy.19
  3.0 0.1 reshape.184
  3.2 0.1 copy.20
  3.3 0.0 copy-done
  3.3 0.8 gather_fusion
  4.1 0.7 fusion
  4.8 1.2 select_maximum_fusion.src_ref
  6.0 54.6 %shard_map.64 = f32[64,33,128]{2,1,0:T(8,128)} custom-call(f32[64,33,128]{2,1,0:T(8,128)} %select_maximum_fusion.src_ref), custom_call_target="tpu_custom_call" | custom-call | tf_op jit(solution)/shard_map/pallas_call | solution.py:273
  60.5 0.0 slice-start
  60.6 1.1 convert_reduce_fusion
  61.7 0.1 convert_element_type.46
  61.8 0.0 slice-done
  61.9 0.2 reshape.185
  62.0 0.3 copy.21
  62.3 0.7 fusion.3
  63.0 0.0 copy-start.1
  63.1 0.0 copy-start.2
  63.1 0.2 copy.25
  63.3 1.0 copy-done.1
  64.3 0.0 copy-done.2
  64.3 139.9 %shard_map.65 = f32[256,1024]{1,0:T(8,128)S(1)} custom-call(f32[256,1024]{1,0:T(8,128)S(1)} %bitcast.29, f32[32,256]{1,0:T(8,128)S(1)} %bitcast.30, f32[256,1024]{1,0:T(8,128)S(1)} %copy-done.1), custom_call_target="tpu_custom_call" | custom-call | tf_op jit(solution)/shard_map/pallas_call | solution.py:198
  204.1 1.0 copy.27
  (8 shorter events, 0.1 us)
Async XLA Ops:
  0.0 3.3 %copy-start = (f32[64,16,128]{2,1,0:T(8,128)S(1)}, f32[64,16,128]{2,1,0:T(8,128)}, u32[]{:S(2)}) copy-start(f32[64,16,128]{2,1,0:T(8,128)} %param.10) | copy-start | bytes 1572868
  60.5 1.3 slice-start
  63.0 1.2 copy-start.1
  63.1 1.2 copy-start.2

commit v8 on v7

--- a/solution.py
+++ b/solution.py
@@ -29,7 +29,7 @@
     return filled, local_index, slot_position
 
 
-def contract_kernel(nz, nb, src_ref, mine_ref, residual_ref, out_ref, held, amps_buf,
+def contract_kernel(nz, nb, src_ref, mine_ref, cross_ref, residual_ref, out_ref, held, amps_buf,
                     send_sem, recv_sem, amp_send, amp_recv):
     zl = lax.axis_index("zl")
     c = lax.axis_index("core")
@@ -41,6 +41,9 @@
     has_right = zl < nz - 1
     own = zl * 2 + c
     n_m = amps_buf.shape[0]
+    half = nb // 2
+    side = me // half
+    me_in = lax.rem(me, half)
 
     barrier = pltpu.get_barrier_semaphore()
     pl.semaphore_signal(barrier, 1, device_id=partner, device_id_type=MESH)
@@ -53,12 +56,15 @@
     def _():
         pl.semaphore_signal(barrier, 1, device_id=right, device_id_type=MESH)
 
-    def greet(p, carry):
-        pl.semaphore_signal(barrier, 1, device_id=(zl, c, lax.rem(me + p, nb)), device_id_type=MESH)
-        return carry
-
-    lax.fori_loop(1, nb, greet, 0)
-    peers = nb + has_left.astype(jnp.int32) + has_right.astype(jnp.int32)
+    def near(q):
+        return side * half + lax.rem(me_in + q, half)
+
+    def greet(q, carry):
+        pl.semaphore_signal(barrier, 1, device_id=(zl, c, near(q)), device_id_type=MESH)
+        return carry
+
+    lax.fori_loop(1, half, greet, 0)
+    peers = half + has_left.astype(jnp.int32) + has_right.astype(jnp.int32)
     pl.semaphore_wait(barrier, peers)
 
     my_m = lax.rem(me, n_m)
@@ -74,11 +80,11 @@
             device_id_type=MESH,
         )
 
-    def amp_send_one(p, carry):
-        amp_copy(p, lax.rem(me + p, nb)).start()
-        return carry
-
-    lax.fori_loop(1, nb, amp_send_one, 0)
+    def amp_send_one(q, carry):
+        amp_copy(q, near(q)).start()
+        return carry
+
+    lax.fori_loop(1, half, amp_send_one, 0)
     amps_buf[my_m, my_k] = mine_ref[...]
 
     def copy(src, slot, kind, dev):
@@ -101,12 +107,12 @@
     def _():
         copy(src_ref, own, 2, right).start()
 
-    def amp_wait(p, carry):
-        source = lax.rem(me + nb - p, nb)
+    def amp_wait(q, carry):
+        source = near(half - q)
         pltpu.make_async_remote_copy(
             src_ref=mine_ref,
             dst_ref=amps_buf.at[lax.rem(source, n_m), source // n_m],
-            send_sem=amp_send.at[p],
+            send_sem=amp_send.at[q],
             recv_sem=amp_recv.at[source],
             device_id=(zl, c, source),
             device_id_type=MESH,
@@ -114,8 +120,13 @@
         return carry
 
     def accumulate(slot, block):
-        half = held.shape[1] // amps_buf.shape[1]
-        part = amps_buf[slot // 2, :, pl.ds(lax.rem(slot, 2) * half, half), :]
+        rows_k = held.shape[1] // amps_buf.shape[1]
+        window = pl.ds(lax.rem(slot, 2) * rows_k, rows_k)
+        near_part = amps_buf[slot // 2, :, window, :]
+        far_part = cross_ref[slot // 2, :, window, :]
+        n_k = amps_buf.shape[1]
+        k_side = lax.broadcasted_iota(jnp.int32, near_part.shape, 0) // (n_k // 2)
+        part = jnp.where(k_side == side, near_part, far_part)
         lhs_t = part.reshape(-1, part.shape[-1])
         out_ref[...] += jnp.dot(
             lhs_t.T, block[...], precision=lax.Precision.HIGHEST,
@@ -143,7 +154,7 @@
             def _():
                 copy(held.at[s], s, 1, left).start()
 
-    lax.fori_loop(1, nb, amp_wait, 0)
+    lax.fori_loop(1, half, amp_wait, 0)
     out_ref[...] = residual_ref[...]
     accumulate(own, src_ref)
     for z in range(nz):
@@ -185,20 +196,20 @@
         def _():
             copy(held.at[s], s, 2, right).wait_send()
 
-    def amp_sent(p, carry):
-        amp_copy(p, lax.rem(me + p, nb)).wait_send()
-        return carry
-
-    lax.fori_loop(1, nb, amp_sent, 0)
-
-
-def gather_contract(placed, mine_t, residual, nz, nb, n_m):
+    def amp_sent(q, carry):
+        amp_copy(q, near(q)).wait_send()
+        return carry
+
+    lax.fori_loop(1, half, amp_sent, 0)
+
+
+def gather_contract(placed, mine_t, cross, residual, nz, nb, n_m):
     groups = 2 * nz
     n_k = nb // n_m
     return pl.pallas_call(
         functools.partial(contract_kernel, nz, nb),
         out_shape=jax.ShapeDtypeStruct(residual.shape, jnp.float32),
-        in_specs=[pl.BlockSpec(memory_space=pltpu.VMEM)] * 3,
+        in_specs=[pl.BlockSpec(memory_space=pltpu.VMEM)] * 4,
         out_specs=pl.BlockSpec(memory_space=pltpu.VMEM),
         scratch_shapes=[
             pltpu.VMEM((groups,) + placed.shape, jnp.float32),
@@ -211,14 +222,21 @@
         compiler_params=pltpu.CompilerParams(
             collective_id=0, has_side_effects=True, vmem_limit_bytes=48 * 1024 * 1024
         ),
-    )(placed, mine_t, residual)
-
-
-def exchange_kernel(nb, src_ref, out_ref, local_sem, send_sem, recv_sem):
+    )(placed, mine_t, cross, residual)
+
+
+def exchange_kernel(nb, n_m, src_ref, mine_ref, out_ref, cross_ref, local_sem, send_sem, recv_sem,
+                    amp_send, amp_recv):
     zl = lax.axis_index("zl")
     c = lax.axis_index("core")
     me = lax.axis_index("bulk")
 
+    half = nb // 2
+    far_side = 1 - me // half
+    me_in = lax.rem(me, half)
+    my_m = lax.rem(me, n_m)
+    my_k = me // n_m
+    cross_ref[...] = jnp.zeros_like(cross_ref)
     barrier = pltpu.get_barrier_semaphore()
 
     def greet(p, carry):
@@ -246,6 +264,25 @@
         return carry
 
     lax.fori_loop(1, nb, send, 0)
+
+    def far(q):
+        return far_side * half + lax.rem(me_in + q, half)
+
+    def amp_copy(q, dest):
+        return pltpu.make_async_remote_copy(
+            src_ref=mine_ref,
+            dst_ref=cross_ref.at[my_m, my_k],
+            send_sem=amp_send.at[q],
+            recv_sem=amp_recv.at[me],
+            device_id=(zl, c, dest),
+            device_id_type=MESH,
+        )
+
+    def amp_send_one(q, carry):
+        amp_copy(q, far(q)).start()
+        return carry
+
+    lax.fori_loop(0, half, amp_send_one, 0)
 
     def receive(p, carry):
         source = lax.rem(me + nb - p, nb)
@@ -262,6 +299,26 @@
     lax.fori_loop(1, nb, receive, 0)
     mine.wait()
 
+    def amp_wait(q, carry):
+        source = far(half - q)
+        pltpu.make_async_remote_copy(
+            src_ref=mine_ref,
+            dst_ref=cross_ref.at[lax.rem(source, n_m), source // n_m],
+            send_sem=amp_send.at[q],
+            recv_sem=amp_recv.at[source],
+            device_id=(zl, c, source),
+            device_id_type=MESH,
+        ).wait_recv()
+        return carry
+
+    lax.fori_loop(0, half, amp_wait, 0)
+
+    def amp_sent(q, carry):
+        amp_copy(q, far(q)).wait_send()
+        return carry
+
+    lax.fori_loop(0, half, amp_sent, 0)
+
     def sent(p, carry):
         copy(p, lax.rem(me + p, nb)).wait_send()
         return carry
@@ -269,19 +326,24 @@
     lax.fori_loop(1, nb, sent, 0)
 
 
-def bulk_exchange(outgoing, nb):
+def bulk_exchange(outgoing, mine_t, nb, n_m):
     return pl.pallas_call(
-        functools.partial(exchange_kernel, nb),
-        out_shape=jax.ShapeDtypeStruct(outgoing.shape, outgoing.dtype),
-        in_specs=[pl.BlockSpec(memory_space=pltpu.VMEM)],
-        out_specs=pl.BlockSpec(memory_space=pltpu.VMEM),
+        functools.partial(exchange_kernel, nb, n_m),
+        out_shape=(
+            jax.ShapeDtypeStruct(outgoing.shape, outgoing.dtype),
+            jax.ShapeDtypeStruct((n_m, nb // n_m) + mine_t.shape, jnp.float32),
+        ),
+        in_specs=[pl.BlockSpec(memory_space=pltpu.VMEM)] * 2,
+        out_specs=(pl.BlockSpec(memory_space=pltpu.VMEM), pl.BlockSpec(memory_space=pltpu.VMEM)),
         scratch_shapes=[
             pltpu.SemaphoreType.DMA(()),
             pltpu.SemaphoreType.DMA((nb,)),
             pltpu.SemaphoreType.DMA((nb,)),
+            pltpu.SemaphoreType.DMA((nb,)),
+            pltpu.SemaphoreType.DMA((nb,)),
         ],
         compiler_params=pltpu.CompilerParams(collective_id=1, has_side_effects=True),
-    )(outgoing)
+    )(outgoing, mine_t)
 
 
 def local(residual_in, amplitudes, integral_tiles, tile_reader, tile_k, tile_column):
@@ -296,15 +358,17 @@
         slot_position.reshape(targets, SLOT).astype(jnp.float32)
     )
     outgoing = jnp.concatenate([picked.reshape(targets, SLOT * height, width), label], axis=1)
-    arrived = bulk_exchange(outgoing, targets)
+    rows, own_cols = amplitudes.shape
+    n_m = width // own_cols
+    mine_t = amplitudes.T
+    arrived, cross = bulk_exchange(outgoing, mine_t, targets, n_m)
     position = arrived[:, SLOT * height, :SLOT].reshape(-1).astype(jnp.int32)
     arrived = arrived[:, : SLOT * height, :].reshape(targets * SLOT, height * width)
     table = (position[None, :] == jnp.arange(KT * CT, dtype=jnp.int32)[:, None]).astype(jnp.float32)
     placed = jnp.dot(table, arrived, precision=lax.Precision.HIGHEST)
     placed = placed.reshape(KT, CT, height, width).transpose(0, 2, 1, 3).reshape(KT * height, CT * width)
     nz = lax.axis_size("zl")
-    rows, own_cols = amplitudes.shape
-    return gather_contract(placed, amplitudes.T, residual_in, nz, targets, width // own_cols)
+    return gather_contract(placed, mine_t, cross, residual_in, nz, targets, n_m)
 
 
 def solution(mesh):

time: 207 us -> 207 us (level)
    pallas_call x1, Pallas kernels: 140 us -> 92 us  [gather_contract(): pl.pallas_call(functools.partial(contract_kernel, nz, nb), out_shape=jax....]
    pallas_call x1, Pallas kernels: 54.6 us -> 101 us  [bulk_exchange(): pl.pallas_call(functools.partial(exchange_kernel, nb, n_m), out_shape=(ja...]
where the time goes in v8:
time: 207 us; the launch traced here: 206 us
  Pallas kernels  193 us (93%)
  local copies, waits for them, and re-layouts  5.87 us (3%)
  other arithmetic  5.61 us (3%)
    pallas_call x1, Pallas kernels, bulk_exchange(): pl.pallas_call(functools.partial(exchange_kernel, nb, n_m), out_shape=(ja...  101 us
    pallas_call x1, Pallas kernels, gather_contract(): pl.pallas_call(functools.partial(contract_kernel, nz, nb), out_shape=jax....  92 us

profile of v8, /device:TPU:6, one launch (start us, length us, event | category | flops | bytes accessed | tf_op | source)
XLA Modules:
  0.0 205.7 jit_solution(634400064210929657)
XLA Ops:
  0.0 0.0 copy-start
  0.0 0.7 multiply_add_fusion.1
  0.7 0.8 fusion.9
  1.5 0.1 reduce_window_sum.11
  1.6 0.8 select_reduce_fusion
  2.5 0.2 fusion.1
  2.7 0.1 copy.18
  2.8 0.1 copy.17
  2.9 0.1 copy.19
  3.0 0.1 reshape.184
  3.2 0.1 copy.20
  3.3 0.0 copy-done
  3.3 0.8 gather_fusion
  4.1 0.7 fusion
  4.8 1.2 select_maximum_fusion.src_ref
  5.9 101.4 %shard_map.64 = (f32[64,33,128]{2,1,0:T(8,128)}, f32[4,16,32,256]{3,2,1,0:T(8,128)}) custom-call(f32[64,33,128]{2,1,0:T(8,128)} %select_maximum_fusion.src_ref, f32[32,256]{1,0:T(8,128)} %bitcast.30), custom_call_target="tpu_custom_call" | custom-call | tf_op jit(solution)/shard_map/pallas_call | solution.py:330
  107.3 1.1 convert_reduce_fusion
  108.4 1.3 slice.30
  109.7 0.1 convert_element_type.46
  109.8 0.2 reshape.185
  110.0 0.3 copy.21
  110.3 0.0 copy-start.2
  110.4 0.0 copy-start.3
  110.4 0.7 fusion.3
  111.1 0.0 copy-start.1
  111.1 0.2 copy.25
  111.3 0.3 copy-done.2
  111.6 0.0 copy-done.3
  111.6 1.2 copy-done.1
  112.7 92.0 %shard_map.65 = f32[256,1024]{1,0:T(8,128)S(1)} custom-call(f32[256,1024]{1,0:T(8,128)S(1)} %bitcast.29, f32[32,256]{1,0:T(8,128)S(1)} %bitcast.31, f32[4,16,32,256]{3,2,1,0:T(8,128)S(1)} %copy-done.1, f32[256,1024]{1,0:T(8,128)S(1)} %copy-done.2), custom_call_target="tpu_custom_call" | custom-call | tf_op jit(solution)/shard_map/pallas_call | solution.py:209
  204.8 1.0 copy.27
  (8 shorter events, 0.1 us)
Async XLA Ops:
  0.0 3.3 %copy-start = (f32[64,16,128]{2,1,0:T(8,128)S(1)}, f32[64,16,128]{2,1,0:T(8,128)}, u32[]{:S(2)}) copy-start(f32[64,16,128]{2,1,0:T(8,128)} %param.10) | copy-start | bytes 1572868
  110.3 1.2 copy-start.2
  110.4 1.2 copy-start.3
  111.1 1.7 copy-start.1

commit v9 on v5

--- a/solution.py
+++ b/solution.py
@@ -13,6 +13,7 @@
 KT = 16
 CT = 8
 SLOT = 2
+Z_HALVES = 2
 
 
 def bucket_slots(tile_reader, tile_k, tile_column, targets, slots):
@@ -32,10 +33,11 @@
 def gather_kernel(nz, src_ref, out_ref, local_sem, send_sem, recv_sem):
     zl = lax.axis_index("zl")
     c = lax.axis_index("core")
-    b = lax.axis_index("bulk")
-    partner = (zl, 1 - c, b)
-    left = (zl - 1, c, b)
-    right = (zl + 1, c, b)
+    zh = lax.axis_index("zh")
+    xy = lax.axis_index("xy")
+    partner = (zl, 1 - c, zh, xy)
+    left = (zl - 1, c, zh, xy)
+    right = (zl + 1, c, zh, xy)
     has_left = zl > 0
     has_right = zl < nz - 1
     own = zl * 2 + c
@@ -131,15 +133,18 @@
     )(placed)
 
 
-def exchange_kernel(nb, src_ref, out_ref, local_sem, send_sem, recv_sem):
+def exchange_kernel(nb, nxy, src_ref, out_ref, local_sem, send_sem, recv_sem):
     zl = lax.axis_index("zl")
     c = lax.axis_index("core")
-    me = lax.axis_index("bulk")
+    me = lax.axis_index("zh") * nxy + lax.axis_index("xy")
+
+    def peer(b):
+        return (zl, c, b // nxy, lax.rem(b, nxy))
 
     barrier = pltpu.get_barrier_semaphore()
 
     def greet(p, carry):
-        pl.semaphore_signal(barrier, 1, device_id=(zl, c, lax.rem(me + p, nb)), device_id_type=MESH)
+        pl.semaphore_signal(barrier, 1, device_id=peer(lax.rem(me + p, nb)), device_id_type=MESH)
         return carry
 
     lax.fori_loop(1, nb, greet, 0)
@@ -154,7 +159,7 @@
             dst_ref=out_ref.at[me],
             send_sem=send_sem.at[p],
             recv_sem=recv_sem.at[me],
-            device_id=(zl, c, dest),
+            device_id=peer(dest),
             device_id_type=MESH,
         )
 
@@ -171,7 +176,7 @@
             dst_ref=out_ref.at[source],
             send_sem=send_sem.at[p],
             recv_sem=recv_sem.at[source],
-            device_id=(zl, c, source),
+            device_id=peer(source),
             device_id_type=MESH,
         ).wait_recv()
         return carry
@@ -186,9 +191,9 @@
     lax.fori_loop(1, nb, sent, 0)
 
 
-def bulk_exchange(outgoing, nb):
+def bulk_exchange(outgoing, nb, nxy):
     return pl.pallas_call(
-        functools.partial(exchange_kernel, nb),
+        functools.partial(exchange_kernel, nb, nxy),
         out_shape=jax.ShapeDtypeStruct(outgoing.shape, outgoing.dtype),
         in_specs=[pl.BlockSpec(memory_space=pltpu.VMEM)],
         out_specs=pl.BlockSpec(memory_space=pltpu.VMEM),
@@ -202,7 +207,8 @@
 
 
 def local(residual_in, amplitudes, integral_tiles, tile_reader, tile_k, tile_column):
-    targets = lax.axis_size("bulk")
+    nxy = lax.axis_size("xy")
+    targets = lax.axis_size("zh") * nxy
     height, width = integral_tiles.shape[1], integral_tiles.shape[2]
     filled, local_index, slot_position = bucket_slots(
         tile_reader, tile_k, tile_column, targets, SLOT
@@ -213,7 +219,7 @@
         slot_position.reshape(targets, SLOT).astype(jnp.float32)
     )
     outgoing = jnp.concatenate([picked.reshape(targets, SLOT * height, width), label], axis=1)
-    arrived = bulk_exchange(outgoing, targets)
+    arrived = bulk_exchange(outgoing, targets, nxy)
     position = arrived[:, SLOT * height, :SLOT].reshape(-1).astype(jnp.int32)
     arrived = arrived[:, : SLOT * height, :].reshape(targets * SLOT, height * width)
     table = (position[None, :] == jnp.arange(KT * CT, dtype=jnp.int32)[:, None]).astype(jnp.float32)
@@ -222,8 +228,10 @@
     nz = lax.axis_size("zl")
     gathered = row_gather(placed, nz)
     dense = gathered.reshape(-1, CT * width)
-    amps = lax.all_gather(amplitudes, "bulk", axis=1, tiled=True)
-    rows = amps.shape[0]
+    pair = lax.all_gather(amplitudes, "zh", axis=0, tiled=False)
+    blocks = lax.all_gather(pair, "xy", axis=0, tiled=False)
+    rows, own_cols = amplitudes.shape
+    amps = blocks.transpose(2, 1, 0, 3).reshape(rows, targets * own_cols)
     groups = gathered.shape[0]
     amps = amps.reshape(rows, KT, groups, height).transpose(0, 2, 1, 3).reshape(rows, -1)
     return residual_in + jnp.dot(amps, dense, precision=lax.Precision.HIGH)
@@ -231,17 +239,19 @@
 
 def solution(mesh):
     row_size = mesh.shape["row"]
-    devices = np.asarray(mesh.devices).reshape(row_size // 2, 2, mesh.shape["bulk"])
-    inner = Mesh(devices, ("zl", "core", "bulk"))
+    bulk_size = mesh.shape["bulk"]
+    devices = np.asarray(mesh.devices).reshape(row_size // 2, 2, Z_HALVES, bulk_size // Z_HALVES)
+    inner = Mesh(devices, ("zl", "core", "zh", "xy"))
     row = ("zl", "core")
+    bulk = ("zh", "xy")
     placed = (
-        P(row, "bulk"),
-        P(row, "bulk"),
-        P("bulk", row, None),
-        P("bulk", None),
-        P("bulk"),
-        P("bulk"),
+        P(row, bulk),
+        P(row, bulk),
+        P(bulk, row, None),
+        P(bulk, None),
+        P(bulk),
+        P(bulk),
     )
     return jax.shard_map(
-        local, mesh=inner, in_specs=placed, out_specs=P(row, "bulk"), check_vma=False
-    )
+        local, mesh=inner, in_specs=placed, out_specs=P(row, bulk), check_vma=False
+    )

time: 202 us -> 184 us (0.911)
  the two profiles are of different devices: /device:TPU:66 before, /device:TPU:6 now
where the time goes in v9:
time: 184 us; the launch traced here: 183 us
  Pallas kernels  134 us (73%)
  between operations  13.6 us (7%)
  blocking collectives  12 us (7%)
  local copies, waits for them, and re-layouts  10.7 us (6%)
  matrix products  7.65 us (4%)
  other arithmetic  5.56 us (3%)
    pallas_call x1, Pallas kernels, row_gather(): pl.pallas_call(functools.partial(gather_kernel, nz), out_shape=jax.ShapeD...  85.5 us
    pallas_call x1, Pallas kernels, bulk_exchange(): pl.pallas_call(functools.partial(exchange_kernel, nb, nxy), out_shape=jax...  48.4 us
    all_gather x1, blocking collectives, local(): pair = lax.all_gather(amplitudes, 'zh', axis=0, tiled=False)  12 us
    dot_general x1, matrix products, local(): return residual_in + jnp.dot(amps, dense, precision=lax.Precision.HIGH)  6.96 us
  transfers between devices with their start and end apart: 1, of which 0 were waited for; matrix products, arithmetic and copies ran while one was open for 6% of the time, Pallas kernels for 73%

profile of v9, /device:TPU:6, one launch (start us, length us, event | category | flops | bytes accessed | tf_op | source)
XLA Modules:
  0.0 183.4 jit_solution(6531563391879925601)
XLA Ops:
  6.5 0.0 copy-start
  6.5 0.0 all-gather.4.cloned.1.call-start
  6.5 12.0 %all-gather = f32[512,32]{0,1:T(8,128)S(1)} all-gather(f32[256,32]{0,1:T(8,128)} %param.9), channel_id=2, replica_groups=mesh['zl'=4,'core'=2,'zh'=2,'xy'=32] {'zh'}, dimensions={0}, use_global_device_ids=true | all-gather | bytes 98304 | tf_op jit(solution)/shard_map/all_gather | solution.py:231
  18.5 0.6 copy.67
  19.1 0.0 all-gather.4.cloned.1.call-update
  19.2 0.8 fusion.10
  20.0 0.1 reduce_window_sum.11
  20.1 0.8 select_reduce_fusion
  20.9 0.7 multiply_add_fusion.1
  21.6 0.2 fusion.2
  21.8 0.1 copy.53
  21.9 0.1 copy.52
  22.0 0.1 copy.51
  22.1 0.1 reshape.190
  22.3 0.1 copy.54
  22.4 0.0 copy-done
  22.4 0.8 gather_fusion
  23.2 0.7 fusion.1
  23.9 1.2 select_maximum_fusion.src_ref
  25.1 48.4 %shard_map.64 = f32[64,33,128]{2,1,0:T(8,128)} custom-call(f32[64,33,128]{2,1,0:T(8,128)} %select_maximum_fusion.src_ref), custom_call_target="tpu_custom_call" | custom-call | tf_op jit(solution)/shard_map/pallas_call | solution.py:195
  73.5 1.3 slice.30
  74.8 1.1 convert_reduce_fusion
  75.8 0.1 convert_element_type.46
  76.0 0.2 reshape.191
  76.1 0.3 copy.55
  76.5 0.0 copy-start.2
  76.5 0.7 fusion.4
  77.2 1.2 copy.66
  78.3 0.0 copy-done.2
  78.3 0.3 copy.59
  78.7 85.5 %shard_map.65 = f32[8,256,1024]{2,1,0:T(8,128)} custom-call(f32[256,1024]{1,0:T(8,128)} %bitcast.49), custom_call_target="tpu_custom_call" | custom-call | tf_op jit(solution)/shard_map/pallas_call | solution.py:122
  164.2 0.0 all-gather.4.cloned.1.call-done
  164.3 0.0 copy-start.1
  164.3 1.9 %copy.57 = f32[256,2,32,32]{0,3,2,1:T(8,128)S(1)} copy(f32[256,2,32,32]{0,3,1,2:T(8,128)} %bitcast.54) | data formatting | bytes 4194304 | tf_op jit(solution)/shard_map/transpose | solution.py:234
  166.2 0.2 copy.58
  166.4 1.9 %copy-done.1 = f32[8,256,1024]{2,1,0:T(8,128)S(1)} copy-done((f32[8,256,1024]{2,1,0:T(8,128)S(1)}, f32[8,256,1024]{2,1,0:T(8,128)}, u32[]{:S(2)}) %copy-start.1) | copy-done | bytes 8388632
  168.3 7.0 %fusion = f32[256,1024]{0,1:T(8,128)S(1)} fusion(f32[256,1024]{0,1:T(8,128)S(1)} %copy.59, f32[2048,1024]{1,0:T(8,128)S(1)} %bitcast.46, f32[256,2048]{0,1:T(8,128)S(1)} %bitcast.48), kind=kOutput, calls=%fused_computation.4 | convolution fusion | flops 3221487616 | bytes 12582912 | tf_op jit(solution)/shard_map/dot_general | solution.py:237
  175.2 1.3 copy.60
  (8 shorter events, 0.1 us)
Async XLA Ops:
  6.5 15.9 %copy-start = (f32[64,16,128]{2,1,0:T(8,128)S(1)}, f32[64,16,128]{2,1,0:T(8,128)}, u32[]{:S(2)}) copy-start(f32[64,16,128]{2,1,0:T(8,128)} %param.10) | copy-start | bytes 1572868
  6.5 157.7 %all-gather.4.cloned.1.call-start = ((), (), s32[]{:S(2)}) async-start(), calls=%async_computation | async-start | bytes 2162688 | tf_op jit(solution)/shard_map/all_gather | solution.py:232
  76.5 1.9 %copy-start.2 = (f32[256,1024]{1,0:T(8,128)S(1)}, f32[256,1024]{1,0:T(8,128)}, u32[]{:S(2)}) copy-start(f32[256,1024]{1,0:T(8,128)} %param.8) | copy-start | bytes 3145732
  164.3 4.0 %copy-start.1 = (f32[8,256,1024]{2,1,0:T(8,128)S(1)}, f32[8,256,1024]{2,1,0:T(8,128)}, u32[]{:S(2)}) copy-start(f32[8,256,1024]{2,1,0:T(8,128)} %shard_map.65) | copy-start | bytes 25165828
Sparse Core Ops, SparseCore 0:
  19.3 90.2 all-gather.3

commit v10 on v9

--- a/solution.py
+++ b/solution.py
@@ -228,8 +228,11 @@
     nz = lax.axis_size("zl")
     gathered = row_gather(placed, nz)
     dense = gathered.reshape(-1, CT * width)
-    pair = lax.all_gather(amplitudes, "zh", axis=0, tiled=False)
+    halves = lax.axis_size("zh")
+    other = lax.ppermute(amplitudes, "zh", perm=[(h, (h + 1) % halves) for h in range(halves)])
+    pair = jnp.stack([amplitudes, other])
     blocks = lax.all_gather(pair, "xy", axis=0, tiled=False)
+    blocks = jnp.where(lax.axis_index("zh") == 0, blocks, blocks[:, ::-1])
     rows, own_cols = amplitudes.shape
     amps = blocks.transpose(2, 1, 0, 3).reshape(rows, targets * own_cols)
     groups = gathered.shape[0]

time: 184 us -> 185 us (level)
  blocking collectives: 12 us -> 0 us
  starting transfers between devices: 0.01 us -> 11 us
  other arithmetic: 5.56 us -> 9.65 us
  local copies, waits for them, and re-layouts: 10.7 us -> 7.75 us
  waiting for transfers between devices: 0.04 us -> 2.16 us
  matrix products: 7.65 us -> 5.8 us
    all_gather x1 -> x0, blocking collectives: 12 us -> none  [local(): pair = lax.all_gather(amplitudes, 'zh', axis=0, tiled=False)]
    ppermute x0 -> x1, starting transfers between devices: none -> 11 us  [local(): lax.ppermute(amplitudes, 'zh', perm=[(h, (h + 1) % halves) for h in range...]
    transpose x0 -> x1, other arithmetic: none -> 2.71 us  [local(): amps = blocks.transpose(2, 1, 0, 3).reshape(rows, targets * own_cols)]
    ppermute x0 -> x1, waiting for transfers between devices: none -> 2.12 us  [local(): lax.ppermute(amplitudes, 'zh', perm=[(h, (h + 1) % halves) for h in range...]
    dot_general x1, matrix products: 6.96 us -> 5.11 us  [local(): return residual_in + jnp.dot(amps, dense, precision=lax.Precision.HIGH)]
    unnamed x8 -> x7, local copies, waits for them, and re-layouts: 3.43 us -> 4.1 us
  transfers between devices with their start and end apart: 1 -> 2, of which waited for: 0 -> 1; matrix products, arithmetic and copies ran while one was open for 6% -> 6% of each run, Pallas kernels for 73% -> 73%
where the time goes in v10:
time: 185 us; the launch traced here: 184 us
  Pallas kernels  134 us (72%)
  between operations  13.6 us (7%)
  starting transfers between devices  11 us (6%)
  other arithmetic  9.65 us (5%)
  local copies, waits for them, and re-layouts  7.75 us (4%)
  matrix products  5.8 us (3%)
  waiting for transfers between devices  2.16 us (1%)
    pallas_call x1, Pallas kernels, row_gather(): pl.pallas_call(functools.partial(gather_kernel, nz), out_shape=jax.ShapeD...  85.7 us
    pallas_call x1, Pallas kernels, bulk_exchange(): pl.pallas_call(functools.partial(exchange_kernel, nb, nxy), out_shape=jax...  48.3 us
    ppermute x1, starting transfers between devices, local(): lax.ppermute(amplitudes, 'zh', perm=[(h, (h + 1) % halves) for h in range...  11 us
    dot_general x1, matrix products, local(): return residual_in + jnp.dot(amps, dense, precision=lax.Precision.HIGH)  5.11 us
    unnamed x7, local copies, waits for them, and re-layouts  4.1 us
  transfers between devices with their start and end apart: 2, of which 1 were waited for; matrix products, arithmetic and copies ran while one was open for 6% of the time, Pallas kernels for 73%

profile of v10, /device:TPU:6, one launch (start us, length us, event | category | flops | bytes accessed | tf_op | source)
XLA Modules:
  0.0 184.0 jit_solution(10198648801882522812)
XLA Ops:
  6.5 0.0 copy-start
  6.5 0.0 all-gather.3.cloned.1.call-start
  6.5 11.0 %collective-permute-start = (f32[256,32]{0,1:T(8,128)}, f32[256,32]{0,1:T(8,128)S(1)}, u32[]{:S(2)}, u32[]{:S(2)}) collective-permute-start(f32[256,32]{0,1:T(8,128)} %param.9), channel_id=1, source_target_pairs={{0,32},{32,0},{1,33},{33,1},{2,34},{34,2},{3,35},{35,3},{4,36},{36... | collective-permute-start | bytes 98312 | tf_op jit(solution)/shard_map/ppermute | solution.py:232
  17.6 2.1 %collective-permute-done = f32[256,32]{0,1:T(8,128)S(1)} collective-permute-done((f32[256,32]{0,1:T(8,128)}, f32[256,32]{0,1:T(8,128)S(1)}, u32[]{:S(2)}, u32[]{:S(2)}) %collective-permute-start) | collective-permute-done | bytes 32800 | tf_op jit(solution)/shard_map/ppermute | solution.py:232
  19.7 1.4 pad_maximum_fusion
  21.1 0.0 all-gather.3.cloned.1.call-update
  21.1 0.8 fusion.10
  21.9 0.1 reduce_window_sum.11
  22.0 0.8 select_reduce_fusion
  22.9 0.7 multiply_add_fusion.1
  23.5 0.2 fusion.2
  23.7 0.1 copy.36
  23.9 0.1 copy.35
  24.0 0.1 copy.34
  24.1 0.1 reshape.191
  24.2 0.1 copy.37
  24.3 0.0 copy-done
  24.3 0.8 gather_fusion
  25.1 0.7 fusion.1
  25.8 1.2 select_maximum_fusion.src_ref
  27.0 48.3 %shard_map.64 = f32[64,33,128]{2,1,0:T(8,128)} custom-call(f32[64,33,128]{2,1,0:T(8,128)} %select_maximum_fusion.src_ref), custom_call_target="tpu_custom_call" | custom-call | tf_op jit(solution)/shard_map/pallas_call | solution.py:195
  75.3 1.3 slice.30
  76.6 1.1 convert_reduce_fusion
  77.7 0.1 convert_element_type.46
  77.8 0.2 reshape.192
  78.0 0.3 copy.38
  78.3 0.7 fusion.4
  79.0 1.2 copy.42
  80.2 85.7 %shard_map.65 = f32[8,256,1024]{2,1,0:T(8,128)} custom-call(f32[256,1024]{1,0:T(8,128)} %bitcast.43), custom_call_target="tpu_custom_call" | custom-call | tf_op jit(solution)/shard_map/pallas_call | solution.py:122
  165.9 0.0 all-gather.3.cloned.1.call-done
  165.9 0.0 copy-start.2
  165.9 2.7 %fusion = f32[256,2,32,32]{0,3,1,2:T(8,128)S(1)} fusion(f32[32,2,256,32]{2,3,1,0:T(8,128)} %bitcast.48, pred[]{:T(512)S(6)} %eq.71), kind=kLoop, calls=%fused_computation.2 | loop fusion | flops 524288 | bytes 4194305 | tf_op jit(solution)/shard_map/transpose | solution.py:237
  168.6 0.0 copy-start.1
  168.7 0.2 copy.32
  168.9 0.2 copy.33
  169.1 0.0 copy-done.2
  169.1 2.9 %copy-done.1 = f32[8,256,1024]{2,1,0:T(8,128)S(1)} copy-done((f32[8,256,1024]{2,1,0:T(8,128)S(1)}, f32[8,256,1024]{2,1,0:T(8,128)}, u32[]{:S(2)}) %copy-start.1) | copy-done | bytes 8388632
  172.0 5.1 %convolution_add_fusion = f32[256,1024]{1,0:T(8,128)} fusion(f32[256,1024]{1,0:T(8,128)S(1)} %copy-done.2, f32[256,2048]{0,1:T(8,128)S(1)} %bitcast.42, f32[2048,1024]{1,0:T(8,128)S(1)} %bitcast.40), kind=kOutput, calls=%fused_computation.5 | convolution fusion | flops 3221487616 | bytes 12582912 | tf_op jit(solution)/shard_map/dot_general | solution.py:240
  (8 shorter events, 0.1 us)
Async XLA Ops:
  6.5 17.8 %copy-start = (f32[64,16,128]{2,1,0:T(8,128)S(1)}, f32[64,16,128]{2,1,0:T(8,128)}, u32[]{:S(2)}) copy-start(f32[64,16,128]{2,1,0:T(8,128)} %param.10) | copy-start | bytes 1572868
  6.5 159.4 %all-gather.3.cloned.1.call-start = ((), (), s32[]{:S(2)}) async-start(), calls=%async_computation | async-start | bytes 2162688 | tf_op jit(solution)/shard_map/all_gather | solution.py:234
  6.5 13.2 %collective-permute-start = (f32[256,32]{0,1:T(8,128)}, f32[256,32]{0,1:T(8,128)S(1)}, u32[]{:S(2)}, u32[]{:S(2)}) collective-permute-start(f32[256,32]{0,1:T(8,128)} %param.9), channel_id=1, source_target_pairs={{0,32},{32,0},{1,33},{33,1},{2,34},{34,2},{3,35},{35,3},{4,36},{36... | collective-permute-start | bytes 98312 | tf_op jit(solution)/shard_map/ppermute | solution.py:232
  165.9 3.2 %copy-start.2 = (f32[256,1024]{1,0:T(8,128)S(1)}, f32[256,1024]{1,0:T(8,128)}, u32[]{:S(2)}) copy-start(f32[256,1024]{1,0:T(8,128)} %param.8) | copy-start | bytes 3145732
  168.6 3.4 %copy-start.1 = (f32[8,256,1024]{2,1,0:T(8,128)S(1)}, f32[8,256,1024]{2,1,0:T(8,128)}, u32[]{:S(2)}) copy-start(f32[8,256,1024]{2,1,0:T(8,128)} %shard_map.65) | copy-start | bytes 25165828
Sparse Core Ops, SparseCore 0:
  21.2 90.1 all-gather.2

commit v11 on v9

--- a/solution.py
+++ b/solution.py
@@ -133,7 +133,8 @@
     )(placed)
 
 
-def exchange_kernel(nb, nxy, src_ref, out_ref, local_sem, send_sem, recv_sem):
+def exchange_kernel(nb, nxy, src_ref, mine_ref, out_ref, other_ref, local_sem, send_sem, recv_sem,
+                    pair_sem):
     zl = lax.axis_index("zl")
     c = lax.axis_index("core")
     me = lax.axis_index("zh") * nxy + lax.axis_index("xy")
@@ -168,6 +169,17 @@
         return carry
 
     lax.fori_loop(1, nb, send, 0)
+
+    twin = lax.rem(me + nb // 2, nb)
+    pair_copy = pltpu.make_async_remote_copy(
+        src_ref=mine_ref,
+        dst_ref=other_ref,
+        send_sem=pair_sem.at[0],
+        recv_sem=pair_sem.at[1],
+        device_id=peer(twin),
+        device_id_type=MESH,
+    )
+    pair_copy.start()
 
     def receive(p, carry):
         source = lax.rem(me + nb - p, nb)
@@ -183,6 +195,8 @@
 
     lax.fori_loop(1, nb, receive, 0)
     mine.wait()
+    pair_copy.wait_recv()
+    pair_copy.wait_send()
 
     def sent(p, carry):
         copy(p, lax.rem(me + p, nb)).wait_send()
@@ -191,19 +205,23 @@
     lax.fori_loop(1, nb, sent, 0)
 
 
-def bulk_exchange(outgoing, nb, nxy):
+def bulk_exchange(outgoing, mine_t, nb, nxy):
     return pl.pallas_call(
         functools.partial(exchange_kernel, nb, nxy),
-        out_shape=jax.ShapeDtypeStruct(outgoing.shape, outgoing.dtype),
-        in_specs=[pl.BlockSpec(memory_space=pltpu.VMEM)],
-        out_specs=pl.BlockSpec(memory_space=pltpu.VMEM),
+        out_shape=(
+            jax.ShapeDtypeStruct(outgoing.shape, outgoing.dtype),
+            jax.ShapeDtypeStruct(mine_t.shape, mine_t.dtype),
+        ),
+        in_specs=[pl.BlockSpec(memory_space=pltpu.VMEM)] * 2,
+        out_specs=(pl.BlockSpec(memory_space=pltpu.VMEM), pl.BlockSpec(memory_space=pltpu.VMEM)),
         scratch_shapes=[
             pltpu.SemaphoreType.DMA(()),
             pltpu.SemaphoreType.DMA((nb,)),
             pltpu.SemaphoreType.DMA((nb,)),
+            pltpu.SemaphoreType.DMA((2,)),
         ],
         compiler_params=pltpu.CompilerParams(collective_id=1, has_side_effects=True),
-    )(outgoing)
+    )(outgoing, mine_t)
 
 
 def local(residual_in, amplitudes, integral_tiles, tile_reader, tile_k, tile_column):
@@ -219,7 +237,7 @@
         slot_position.reshape(targets, SLOT).astype(jnp.float32)
     )
     outgoing = jnp.concatenate([picked.reshape(targets, SLOT * height, width), label], axis=1)
-    arrived = bulk_exchange(outgoing, targets, nxy)
+    arrived, other_t = bulk_exchange(outgoing, amplitudes.T, targets, nxy)
     position = arrived[:, SLOT * height, :SLOT].reshape(-1).astype(jnp.int32)
     arrived = arrived[:, : SLOT * height, :].reshape(targets * SLOT, height * width)
     table = (position[None, :] == jnp.arange(KT * CT, dtype=jnp.int32)[:, None]).astype(jnp.float32)
@@ -228,8 +246,9 @@
     nz = lax.axis_size("zl")
     gathered = row_gather(placed, nz)
     dense = gathered.reshape(-1, CT * width)
-    pair = lax.all_gather(amplitudes, "zh", axis=0, tiled=False)
+    pair = jnp.stack([amplitudes, other_t.T])
     blocks = lax.all_gather(pair, "xy", axis=0, tiled=False)
+    blocks = jnp.where(lax.axis_index("zh") == 0, blocks, blocks[:, ::-1])
     rows, own_cols = amplitudes.shape
     amps = blocks.transpose(2, 1, 0, 3).reshape(rows, targets * own_cols)
     groups = gathered.shape[0]

time: 184 us -> 176 us (0.957)
  blocking collectives: 12 us -> 0 us
  Pallas kernels: 134 us -> 139 us
  other arithmetic: 5.56 us -> 9.67 us
  local copies, waits for them, and re-layouts: 10.7 us -> 7.76 us
  matrix products: 7.65 us -> 5.8 us
    all_gather x1 -> x0, blocking collectives: 12 us -> none  [local(): pair = lax.all_gather(amplitudes, 'zh', axis=0, tiled=False)]
    pallas_call x1, Pallas kernels: 48.4 us -> 55.1 us  [bulk_exchange(): pl.pallas_call(functools.partial(exchange_kernel, nb, nxy), out_shape=(ja...]
    transpose x0 -> x1, other arithmetic: none -> 2.71 us  [local(): amps = blocks.transpose(2, 1, 0, 3).reshape(rows, targets * own_cols)]
    pallas_call x1, Pallas kernels: 85.5 us -> 83.6 us  [row_gather(): pl.pallas_call(functools.partial(gather_kernel, nz), out_shape=jax.ShapeD...]
    dot_general x1, matrix products: 6.96 us -> 5.11 us  [local(): return residual_in + jnp.dot(amps, dense, precision=lax.Precision.HIGH)]
    unnamed x8 -> x9, local copies, waits for them, and re-layouts: 3.43 us -> 4.1 us
  transfers between devices with their start and end apart: 1 -> 1, of which waited for: 0 -> 0; matrix products, arithmetic and copies ran while one was open for 6% -> 3% of each run, Pallas kernels for 73% -> 48%
where the time goes in v11:
time: 176 us
  Pallas kernels  139 us (79%)
  between operations  13.6 us (8%)
  other arithmetic  9.67 us (5%)
  local copies, waits for them, and re-layouts  7.76 us (4%)
  matrix products  5.8 us (3%)
    pallas_call x1, Pallas kernels, row_gather(): pl.pallas_call(functools.partial(gather_kernel, nz), out_shape=jax.ShapeD...  83.6 us
    pallas_call x1, Pallas kernels, bulk_exchange(): pl.pallas_call(functools.partial(exchange_kernel, nb, nxy), out_shape=(ja...  55.1 us
    dot_general x1, matrix products, local(): return residual_in + jnp.dot(amps, dense, precision=lax.Precision.HIGH)  5.11 us
    unnamed x9, local copies, waits for them, and re-layouts  4.1 us
  transfers between devices with their start and end apart: 1, of which 0 were waited for; matrix products, arithmetic and copies ran while one was open for 3% of the time, Pallas kernels for 48%

profile of v11, /device:TPU:6, one launch (start us, length us, event | category | flops | bytes accessed | tf_op | source)
XLA Modules:
  0.0 175.5 jit_solution(2348958532209890433)
XLA Ops:
  6.5 0.0 copy-start
  6.5 0.0 all-gather.3.cloned.1.call-start
  6.5 0.8 fusion.10
  7.3 0.1 reduce_window_sum.11
  7.4 0.8 select_reduce_fusion
  8.3 0.7 multiply_add_fusion.1
  9.0 0.2 fusion.2
  9.2 0.1 copy.35
  9.3 0.1 copy.34
  9.4 0.1 copy.33
  9.5 0.1 reshape.190
  9.7 0.1 copy.36
  9.8 0.0 copy-done
  9.8 0.8 gather_fusion
  10.5 0.7 fusion.1
  11.3 0.0 copy-start.3
  11.3 1.2 select_maximum_fusion.src_ref
  12.5 55.1 %shard_map.64 = (f32[64,33,128]{2,1,0:T(8,128)}, f32[32,256]{1,0:T(8,128)}) custom-call(f32[64,33,128]{2,1,0:T(8,128)} %select_maximum_fusion.src_ref, f32[32,256]{1,0:T(8,128)} %bitcast.52), custom_call_target="tpu_custom_call" | custom-call | tf_op jit(solution)/shard_map/pallas_call | solution.py:209
  67.6 0.0 copy-done.3
  67.6 1.4 pad_maximum_fusion
  69.0 0.0 all-gather.3.cloned.1.call-update
  69.0 1.3 slice.30
  70.3 1.1 convert_reduce_fusion
  71.4 0.1 convert_element_type.46
  71.5 0.2 reshape.192
  71.7 0.3 copy.39
  72.0 0.7 fusion.4
  72.7 1.2 copy.43
  73.9 83.6 %shard_map.65 = f32[8,256,1024]{2,1,0:T(8,128)} custom-call(f32[256,1024]{1,0:T(8,128)} %bitcast.46), custom_call_target="tpu_custom_call" | custom-call | tf_op jit(solution)/shard_map/pallas_call | solution.py:122
  157.4 0.0 all-gather.3.cloned.1.call-done
  157.5 0.0 copy-start.2
  157.5 2.7 %fusion = f32[256,2,32,32]{0,3,1,2:T(8,128)S(1)} fusion(f32[32,2,256,32]{2,3,1,0:T(8,128)} %bitcast.51, pred[]{:T(512)S(6)} %eq.71), kind=kLoop, calls=%fused_computation.2 | loop fusion | flops 524288 | bytes 4194305 | tf_op jit(solution)/shard_map/transpose | solution.py:253
  160.2 0.0 copy-start.1
  160.2 0.2 copy.37
  160.5 0.2 copy.38
  160.7 0.0 copy-done.2
  160.7 2.9 %copy-done.1 = f32[8,256,1024]{2,1,0:T(8,128)S(1)} copy-done((f32[8,256,1024]{2,1,0:T(8,128)S(1)}, f32[8,256,1024]{2,1,0:T(8,128)}, u32[]{:S(2)}) %copy-start.1) | copy-done | bytes 8388632
  163.6 5.1 %convolution_add_fusion = f32[256,1024]{1,0:T(8,128)} fusion(f32[256,1024]{1,0:T(8,128)S(1)} %copy-done.2, f32[256,2048]{0,1:T(8,128)S(1)} %bitcast.45, f32[2048,1024]{1,0:T(8,128)S(1)} %bitcast.43), kind=kOutput, calls=%fused_computation.5 | convolution fusion | flops 3221487616 | bytes 12582912 | tf_op jit(solution)/shard_map/dot_general | solution.py:256
  (8 shorter events, 0.1 us)
Async XLA Ops:
  6.5 3.2 %copy-start = (f32[64,16,128]{2,1,0:T(8,128)S(1)}, f32[64,16,128]{2,1,0:T(8,128)}, u32[]{:S(2)}) copy-start(f32[64,16,128]{2,1,0:T(8,128)} %param.10) | copy-start | bytes 1572868
  6.5 150.9 %all-gather.3.cloned.1.call-start = ((), (), s32[]{:S(2)}) async-start(), calls=%async_computation | async-start | bytes 2162688 | tf_op jit(solution)/shard_map/all_gather | solution.py:250
  11.3 56.3 %copy-start.3 = (f32[256,32]{0,1:T(8,128)S(1)}, f32[256,32]{0,1:T(8,128)}, u32[]{:S(2)}) copy-start(f32[256,32]{0,1:T(8,128)} %param.9) | copy-start | bytes 98308
  157.5 3.2 %copy-start.2 = (f32[256,1024]{1,0:T(8,128)S(1)}, f32[256,1024]{1,0:T(8,128)}, u32[]{:S(2)}) copy-start(f32[256,1024]{1,0:T(8,128)} %param.8) | copy-start | bytes 3145732
  160.2 3.4 %copy-start.1 = (f32[8,256,1024]{2,1,0:T(8,128)S(1)}, f32[8,256,1024]{2,1,0:T(8,128)}, u32[]{:S(2)}) copy-start(f32[8,256,1024]{2,1,0:T(8,128)} %shard_map.65) | copy-start | bytes 25165828
Sparse Core Ops, SparseCore 0:
  69.1 80.5 all-gather.2

commit v12 on v11

--- a/solution.py
+++ b/solution.py
@@ -246,9 +246,10 @@
     nz = lax.axis_size("zl")
     gathered = row_gather(placed, nz)
     dense = gathered.reshape(-1, CT * width)
-    pair = jnp.stack([amplitudes, other_t.T])
+    other = other_t.T
+    lower = lax.axis_index("zh") == 0
+    pair = jnp.stack([jnp.where(lower, amplitudes, other), jnp.where(lower, other, amplitudes)])
     blocks = lax.all_gather(pair, "xy", axis=0, tiled=False)
-    blocks = jnp.where(lax.axis_index("zh") == 0, blocks, blocks[:, ::-1])
     rows, own_cols = amplitudes.shape
     amps = blocks.transpose(2, 1, 0, 3).reshape(rows, targets * own_cols)
     groups = gathered.shape[0]

time: 176 us -> 174 us (0.989)
  other arithmetic: 9.67 us -> 6.97 us
    transpose x1 -> x0, other arithmetic: 2.71 us -> none  [local(): amps = blocks.transpose(2, 1, 0, 3).reshape(rows, targets * own_cols)]
where the time goes in v12:
time: 174 us
  Pallas kernels  139 us (80%)
  between operations  13.6 us (8%)
  local copies, waits for them, and re-layouts  8.38 us (5%)
  other arithmetic  6.97 us (4%)
  matrix products  5.8 us (3%)
    pallas_call x1, Pallas kernels, row_gather(): pl.pallas_call(functools.partial(gather_kernel, nz), out_shape=jax.ShapeD...  83.7 us
    pallas_call x1, Pallas kernels, bulk_exchange(): pl.pallas_call(functools.partial(exchange_kernel, nb, nxy), out_shape=(ja...  55.1 us
    dot_general x1, matrix products, local(): return residual_in + jnp.dot(amps, dense, precision=lax.Precision.HIGH)  5.1 us
  transfers between devices with their start and end apart: 1, of which 0 were waited for; matrix products, arithmetic and copies ran while one was open for 3% of the time, Pallas kernels for 48%

profile of v12, /device:TPU:6, one launch (start us, length us, event | category | flops | bytes accessed | tf_op | source)
XLA Modules:
  0.0 173.6 jit_solution(8184027353133111552)
XLA Ops:
  6.5 0.0 copy-start
  6.5 0.0 all-gather.3.cloned.1.call-start
  6.5 0.8 fusion.11
  7.3 0.1 reduce_window_sum.11
  7.4 0.8 select_reduce_fusion
  8.3 0.7 multiply_add_fusion.1
  9.0 0.2 fusion.1
  9.2 0.1 copy.34
  9.3 0.1 copy.33
  9.4 0.1 copy.32
  9.5 0.1 reshape.190
  9.7 0.1 copy.35
  9.8 0.0 copy-done
  9.8 0.8 gather_fusion
  10.5 0.7 fusion
  11.3 0.0 copy-start.3
  11.3 1.2 select_maximum_fusion.src_ref
  12.5 55.1 %shard_map.64 = (f32[64,33,128]{2,1,0:T(8,128)}, f32[32,256]{1,0:T(8,128)}) custom-call(f32[64,33,128]{2,1,0:T(8,128)} %select_maximum_fusion.src_ref, f32[32,256]{1,0:T(8,128)} %bitcast.59), custom_call_target="tpu_custom_call" | custom-call | tf_op jit(solution)/shard_map/pallas_call | solution.py:209
  67.6 0.0 copy-done.3
  67.6 0.8 fusion.6
  68.4 0.6 pad_maximum_fusion
  69.0 0.0 all-gather.3.cloned.1.call-update
  69.0 1.3 slice.30
  70.3 1.1 convert_reduce_fusion
  71.4 0.1 convert_element_type.46
  71.5 0.2 reshape.192
  71.7 0.3 copy.38
  72.0 0.7 fusion.3
  72.7 1.2 copy.42
  73.9 0.0 copy-start.2
  73.9 83.7 %shard_map.65 = f32[8,256,1024]{2,1,0:T(8,128)} custom-call(f32[256,1024]{1,0:T(8,128)} %bitcast.53), custom_call_target="tpu_custom_call" | custom-call | tf_op jit(solution)/shard_map/pallas_call | solution.py:122
  157.6 0.0 all-gather.3.cloned.1.call-done
  157.6 0.0 copy-start.1
  157.6 1.9 %copy.36 = f32[256,2,32,32]{0,3,2,1:T(8,128)S(1)} copy(f32[256,2,32,32]{0,3,1,2:T(8,128)} %bitcast.58) | data formatting | bytes 4194304 | tf_op jit(solution)/shard_map/transpose | solution.py:254
  159.5 0.2 copy.37
  159.7 0.0 copy-done.2
  159.7 1.9 %copy-done.1 = f32[8,256,1024]{2,1,0:T(8,128)S(1)} copy-done((f32[8,256,1024]{2,1,0:T(8,128)S(1)}, f32[8,256,1024]{2,1,0:T(8,128)}, u32[]{:S(2)}) %copy-start.1) | copy-done | bytes 8388632
  161.6 5.1 %convolution_add_fusion = f32[256,1024]{1,0:T(8,128)} fusion(f32[256,1024]{1,0:T(8,128)S(1)} %copy-done.2, f32[256,2048]{0,1:T(8,128)S(1)} %bitcast.52, f32[2048,1024]{1,0:T(8,128)S(1)} %bitcast.50), kind=kOutput, calls=%fused_computation.3 | convolution fusion | flops 3221487616 | bytes 12582912 | tf_op jit(solution)/shard_map/dot_general | solution.py:257
  (8 shorter events, 0.1 us)
Async XLA Ops:
  6.5 3.2 %copy-start = (f32[64,16,128]{2,1,0:T(8,128)S(1)}, f32[64,16,128]{2,1,0:T(8,128)}, u32[]{:S(2)}) copy-start(f32[64,16,128]{2,1,0:T(8,128)} %param.10) | copy-start | bytes 1572868
  6.5 151.1 %all-gather.3.cloned.1.call-start = ((), (), s32[]{:S(2)}) async-start(), calls=%async_computation | async-start | bytes 2162688 | tf_op jit(solution)/shard_map/all_gather | solution.py:252
  11.3 56.3 %copy-start.3 = (f32[256,32]{0,1:T(8,128)S(1)}, f32[256,32]{0,1:T(8,128)}, u32[]{:S(2)}) copy-start(f32[256,32]{0,1:T(8,128)} %param.9) | copy-start | bytes 98308
  73.9 85.8 %copy-start.2 = (f32[256,1024]{1,0:T(8,128)S(1)}, f32[256,1024]{1,0:T(8,128)}, u32[]{:S(2)}) copy-start(f32[256,1024]{1,0:T(8,128)} %param.8) | copy-start | bytes 3145732
  157.6 4.0 %copy-start.1 = (f32[8,256,1024]{2,1,0:T(8,128)S(1)}, f32[8,256,1024]{2,1,0:T(8,128)}, u32[]{:S(2)}) copy-start(f32[8,256,1024]{2,1,0:T(8,128)} %shard_map.65) | copy-start | bytes 25165828
Sparse Core Ops, SparseCore 0:
  69.1 80.5 all-gather.2

commit v13 on v12

--- a/solution.py
+++ b/solution.py
@@ -14,6 +14,7 @@
 CT = 8
 SLOT = 2
 Z_HALVES = 2
+RELAY_PARTS = 2
 
 
 def bucket_slots(tile_reader, tile_k, tile_column, targets, slots):
@@ -30,7 +31,7 @@
     return filled, local_index, slot_position
 
 
-def gather_kernel(nz, src_ref, out_ref, local_sem, send_sem, recv_sem):
+def gather_kernel(nz, parts, src_ref, out_ref, local_sem, send_sem, recv_sem):
     zl = lax.axis_index("zl")
     c = lax.axis_index("core")
     zh = lax.axis_index("zh")
@@ -56,78 +57,85 @@
     peers = 1 + has_left.astype(jnp.int32) + has_right.astype(jnp.int32)
     pl.semaphore_wait(barrier, peers)
 
-    def copy(src, slot, kind, dev):
+    piece = src_ref.shape[0] // parts
+
+    def copy(src, slot, kind, dev, q):
+        rows = pl.ds(q * piece, piece)
         return pltpu.make_async_remote_copy(
-            src_ref=src,
-            dst_ref=out_ref.at[slot],
-            send_sem=send_sem.at[slot, kind],
-            recv_sem=recv_sem.at[slot],
+            src_ref=src.at[rows],
+            dst_ref=out_ref.at[slot, rows],
+            send_sem=send_sem.at[slot, q, kind],
+            recv_sem=recv_sem.at[slot, q],
             device_id=dev,
             device_id_type=MESH,
         )
 
     mine = pltpu.make_async_copy(src_ref, out_ref.at[own], local_sem)
     mine.start()
-    copy(src_ref, own, 0, partner).start()
-
-    @pl.when(has_left)
-    def _():
-        copy(src_ref, own, 1, left).start()
-
-    @pl.when(has_right)
-    def _():
-        copy(src_ref, own, 2, right).start()
+    for q in range(parts):
+        copy(src_ref, own, 0, partner, q).start()
+
+        @pl.when(has_left)
+        def _():
+            copy(src_ref, own, 1, left, q).start()
+
+        @pl.when(has_right)
+        def _():
+            copy(src_ref, own, 2, right, q).start()
 
     for d in range(1, nz):
-        @pl.when(zl - d >= 0)
-        def _():
-            s = (zl - d) * 2 + c
-            copy(out_ref.at[s], s, 0, partner).wait_recv()
-            copy(out_ref.at[s], s, 0, partner).start()
-
-            @pl.when(has_right)
-            def _():
-                copy(out_ref.at[s], s, 2, right).start()
-
-        @pl.when(zl + d <= nz - 1)
-        def _():
-            s = (zl + d) * 2 + c
-            copy(out_ref.at[s], s, 0, partner).wait_recv()
-            copy(out_ref.at[s], s, 0, partner).start()
-
-            @pl.when(has_left)
-            def _():
-                copy(out_ref.at[s], s, 1, left).start()
+        for q in range(parts):
+            @pl.when(zl - d >= 0)
+            def _():
+                s = (zl - d) * 2 + c
+                copy(out_ref.at[s], s, 0, partner, q).wait_recv()
+                copy(out_ref.at[s], s, 0, partner, q).start()
+
+                @pl.when(has_right)
+                def _():
+                    copy(out_ref.at[s], s, 2, right, q).start()
+
+            @pl.when(zl + d <= nz - 1)
+            def _():
+                s = (zl + d) * 2 + c
+                copy(out_ref.at[s], s, 0, partner, q).wait_recv()
+                copy(out_ref.at[s], s, 0, partner, q).start()
+
+                @pl.when(has_left)
+                def _():
+                    copy(out_ref.at[s], s, 1, left, q).start()
 
     for z in range(nz):
         s = z * 2 + (1 - c)
-        copy(out_ref.at[s], s, 0, partner).wait_recv()
+        for q in range(parts):
+            copy(out_ref.at[s], s, 0, partner, q).wait_recv()
 
     mine.wait()
     for z in range(nz):
         s = z * 2 + c
-        copy(out_ref.at[s], s, 0, partner).wait_send()
-
-        @pl.when(has_left & (z >= zl))
-        def _():
-            copy(out_ref.at[s], s, 1, left).wait_send()
-
-        @pl.when(has_right & (z <= zl))
-        def _():
-            copy(out_ref.at[s], s, 2, right).wait_send()
+        for q in range(parts):
+            copy(out_ref.at[s], s, 0, partner, q).wait_send()
+
+            @pl.when(has_left & (z >= zl))
+            def _():
+                copy(out_ref.at[s], s, 1, left, q).wait_send()
+
+            @pl.when(has_right & (z <= zl))
+            def _():
+                copy(out_ref.at[s], s, 2, right, q).wait_send()
 
 
 def row_gather(placed, nz):
     groups = 2 * nz
     return pl.pallas_call(
-        functools.partial(gather_kernel, nz),
+        functools.partial(gather_kernel, nz, RELAY_PARTS),
         out_shape=jax.ShapeDtypeStruct((groups,) + placed.shape, placed.dtype),
         in_specs=[pl.BlockSpec(memory_space=pltpu.VMEM)],
         out_specs=pl.BlockSpec(memory_space=pltpu.VMEM),
         scratch_shapes=[
             pltpu.SemaphoreType.DMA(()),
-            pltpu.SemaphoreType.DMA((groups, 3)),
-            pltpu.SemaphoreType.DMA((groups,)),
+            pltpu.SemaphoreType.DMA((groups, RELAY_PARTS, 3)),
+            pltpu.SemaphoreType.DMA((groups, RELAY_PARTS)),
         ],
         compiler_params=pltpu.CompilerParams(collective_id=0, has_side_effects=True),
     )(placed)

time: 174 us -> 168 us (0.966)
  Pallas kernels: 139 us -> 133 us
    pallas_call x1, Pallas kernels: 83.7 us -> 77.4 us  [row_gather(): pl.pallas_call(functools.partial(gather_kernel, nz, RELAY_PARTS), out_sha...]
  transfers between devices with their start and end apart: 1 -> 1, of which waited for: 0 -> 0; matrix products, arithmetic and copies ran while one was open for 3% -> 3% of each run, Pallas kernels for 48% -> 46%
where the time goes in v13:
time: 168 us; the launch traced here: 167 us
  Pallas kernels  133 us (79%)
  between operations  13.6 us (8%)
  local copies, waits for them, and re-layouts  8.38 us (5%)
  other arithmetic  6.97 us (4%)
  matrix products  5.8 us (3%)
    pallas_call x1, Pallas kernels, row_gather(): pl.pallas_call(functools.partial(gather_kernel, nz, RELAY_PARTS), out_sha...  77.4 us
    pallas_call x1, Pallas kernels, bulk_exchange(): pl.pallas_call(functools.partial(exchange_kernel, nb, nxy), out_shape=(ja...  55.1 us
    dot_general x1, matrix products, local(): return residual_in + jnp.dot(amps, dense, precision=lax.Precision.HIGH)  5.11 us
  transfers between devices with their start and end apart: 1, of which 0 were waited for; matrix products, arithmetic and copies ran while one was open for 3% of the time, Pallas kernels for 46%

profile of v13, /device:TPU:6, one launch (start us, length us, event | category | flops | bytes accessed | tf_op | source)
XLA Modules:
  0.0 167.3 jit_solution(5407603941761616324)
XLA Ops:
  6.5 0.0 copy-start
  6.5 0.0 all-gather.3.cloned.1.call-start
  6.5 0.8 fusion.11
  7.3 0.1 reduce_window_sum.11
  7.4 0.8 select_reduce_fusion
  8.3 0.7 multiply_add_fusion.1
  9.0 0.2 fusion.1
  9.2 0.1 copy.34
  9.3 0.1 copy.33
  9.4 0.1 copy.32
  9.5 0.1 reshape.190
  9.7 0.1 copy.35
  9.8 0.0 copy-done
  9.8 0.8 gather_fusion
  10.5 0.7 fusion
  11.3 0.0 copy-start.3
  11.3 1.2 select_maximum_fusion.src_ref
  12.5 55.1 %shard_map.64 = (f32[64,33,128]{2,1,0:T(8,128)}, f32[32,256]{1,0:T(8,128)}) custom-call(f32[64,33,128]{2,1,0:T(8,128)} %select_maximum_fusion.src_ref, f32[32,256]{1,0:T(8,128)} %bitcast.59), custom_call_target="tpu_custom_call" | custom-call | tf_op jit(solution)/shard_map/pallas_call | solution.py:217
  67.6 0.0 copy-done.3
  67.6 0.8 fusion.6
  68.4 0.6 pad_maximum_fusion
  69.0 0.0 all-gather.3.cloned.1.call-update
  69.0 1.3 slice.30
  70.3 1.1 convert_reduce_fusion
  71.4 0.1 convert_element_type.46
  71.5 0.2 reshape.192
  71.7 0.3 copy.38
  72.0 0.7 fusion.3
  72.7 1.2 copy.42
  73.9 0.0 copy-start.2
  73.9 77.4 %shard_map.65 = f32[8,256,1024]{2,1,0:T(8,128)} custom-call(f32[256,1024]{1,0:T(8,128)} %bitcast.53), custom_call_target="tpu_custom_call" | custom-call | tf_op jit(solution)/shard_map/pallas_call | solution.py:130
  151.3 0.0 all-gather.3.cloned.1.call-done
  151.3 0.0 copy-start.1
  151.3 1.9 %copy.36 = f32[256,2,32,32]{0,3,2,1:T(8,128)S(1)} copy(f32[256,2,32,32]{0,3,1,2:T(8,128)} %bitcast.58) | data formatting | bytes 4194304 | tf_op jit(solution)/shard_map/transpose | solution.py:262
  153.2 0.2 copy.37
  153.4 0.0 copy-done.2
  153.4 1.9 %copy-done.1 = f32[8,256,1024]{2,1,0:T(8,128)S(1)} copy-done((f32[8,256,1024]{2,1,0:T(8,128)S(1)}, f32[8,256,1024]{2,1,0:T(8,128)}, u32[]{:S(2)}) %copy-start.1) | copy-done | bytes 8388632
  155.3 5.1 %convolution_add_fusion = f32[256,1024]{1,0:T(8,128)} fusion(f32[256,1024]{1,0:T(8,128)S(1)} %copy-done.2, f32[256,2048]{0,1:T(8,128)S(1)} %bitcast.52, f32[2048,1024]{1,0:T(8,128)S(1)} %bitcast.50), kind=kOutput, calls=%fused_computation.3 | convolution fusion | flops 3221487616 | bytes 12582912 | tf_op jit(solution)/shard_map/dot_general | solution.py:265
  (8 shorter events, 0.1 us)
Async XLA Ops:
  6.5 3.2 %copy-start = (f32[64,16,128]{2,1,0:T(8,128)S(1)}, f32[64,16,128]{2,1,0:T(8,128)}, u32[]{:S(2)}) copy-start(f32[64,16,128]{2,1,0:T(8,128)} %param.10) | copy-start | bytes 1572868
  6.5 144.8 %all-gather.3.cloned.1.call-start = ((), (), s32[]{:S(2)}) async-start(), calls=%async_computation | async-start | bytes 2162688 | tf_op jit(solution)/shard_map/all_gather | solution.py:260
  11.3 56.3 %copy-start.3 = (f32[256,32]{0,1:T(8,128)S(1)}, f32[256,32]{0,1:T(8,128)}, u32[]{:S(2)}) copy-start(f32[256,32]{0,1:T(8,128)} %param.9) | copy-start | bytes 98308
  73.9 79.5 %copy-start.2 = (f32[256,1024]{1,0:T(8,128)S(1)}, f32[256,1024]{1,0:T(8,128)}, u32[]{:S(2)}) copy-start(f32[256,1024]{1,0:T(8,128)} %param.8) | copy-start | bytes 3145732
  151.3 4.0 %copy-start.1 = (f32[8,256,1024]{2,1,0:T(8,128)S(1)}, f32[8,256,1024]{2,1,0:T(8,128)}, u32[]{:S(2)}) copy-start(f32[8,256,1024]{2,1,0:T(8,128)} %shard_map.65) | copy-start | bytes 25165828
Sparse Core Ops, SparseCore 0:
  69.1 80.5 all-gather.2

commit v14 on v13

--- a/solution.py
+++ b/solution.py
@@ -14,7 +14,7 @@
 CT = 8
 SLOT = 2
 Z_HALVES = 2
-RELAY_PARTS = 2
+RELAY_PARTS = 4
 
 
 def bucket_slots(tile_reader, tile_k, tile_column, targets, slots):

time: 168 us -> 168 us (level)
  no operation moved by 1% of the time
where the time goes in v14:
time: 168 us
  Pallas kernels  133 us (79%)
  between operations  13.6 us (8%)
  local copies, waits for them, and re-layouts  8.38 us (5%)
  other arithmetic  6.97 us (4%)
  matrix products  5.8 us (3%)
    pallas_call x1, Pallas kernels, row_gather(): pl.pallas_call(functools.partial(gather_kernel, nz, RELAY_PARTS), out_sha...  77.6 us
    pallas_call x1, Pallas kernels, bulk_exchange(): pl.pallas_call(functools.partial(exchange_kernel, nb, nxy), out_shape=(ja...  55.1 us
    dot_general x1, matrix products, local(): return residual_in + jnp.dot(amps, dense, precision=lax.Precision.HIGH)  5.11 us
  transfers between devices with their start and end apart: 1, of which 0 were waited for; matrix products, arithmetic and copies ran while one was open for 3% of the time, Pallas kernels for 46%

profile of v14, /device:TPU:6, one launch (start us, length us, event | category | flops | bytes accessed | tf_op | source)
XLA Modules:
  0.0 167.5 jit_solution(11355488429245810521)
XLA Ops:
  6.5 0.0 copy-start
  6.5 0.0 all-gather.3.cloned.1.call-start
  6.5 0.8 fusion.11
  7.3 0.1 reduce_window_sum.11
  7.4 0.8 select_reduce_fusion
  8.3 0.7 multiply_add_fusion.1
  9.0 0.2 fusion.1
  9.2 0.1 copy.34
  9.3 0.1 copy.33
  9.4 0.1 copy.32
  9.5 0.1 reshape.190
  9.7 0.1 copy.35
  9.8 0.0 copy-done
  9.8 0.8 gather_fusion
  10.5 0.7 fusion
  11.3 0.0 copy-start.3
  11.3 1.2 select_maximum_fusion.src_ref
  12.5 55.1 %shard_map.64 = (f32[64,33,128]{2,1,0:T(8,128)}, f32[32,256]{1,0:T(8,128)}) custom-call(f32[64,33,128]{2,1,0:T(8,128)} %select_maximum_fusion.src_ref, f32[32,256]{1,0:T(8,128)} %bitcast.59), custom_call_target="tpu_custom_call" | custom-call | tf_op jit(solution)/shard_map/pallas_call | solution.py:217
  67.6 0.0 copy-done.3
  67.6 0.8 fusion.6
  68.4 0.6 pad_maximum_fusion
  69.0 0.0 all-gather.3.cloned.1.call-update
  69.0 1.3 slice.30
  70.3 1.1 convert_reduce_fusion
  71.4 0.1 convert_element_type.46
  71.5 0.2 reshape.192
  71.7 0.3 copy.38
  72.0 0.7 fusion.3
  72.7 1.2 copy.42
  73.9 0.0 copy-start.2
  73.9 77.6 %shard_map.65 = f32[8,256,1024]{2,1,0:T(8,128)} custom-call(f32[256,1024]{1,0:T(8,128)} %bitcast.53), custom_call_target="tpu_custom_call" | custom-call | tf_op jit(solution)/shard_map/pallas_call | solution.py:130
  151.5 0.0 all-gather.3.cloned.1.call-done
  151.5 0.0 copy-start.1
  151.5 1.9 %copy.36 = f32[256,2,32,32]{0,3,2,1:T(8,128)S(1)} copy(f32[256,2,32,32]{0,3,1,2:T(8,128)} %bitcast.58) | data formatting | bytes 4194304 | tf_op jit(solution)/shard_map/transpose | solution.py:262
  153.4 0.2 copy.37
  153.6 0.0 copy-done.2
  153.6 1.9 %copy-done.1 = f32[8,256,1024]{2,1,0:T(8,128)S(1)} copy-done((f32[8,256,1024]{2,1,0:T(8,128)S(1)}, f32[8,256,1024]{2,1,0:T(8,128)}, u32[]{:S(2)}) %copy-start.1) | copy-done | bytes 8388632
  155.5 5.1 %convolution_add_fusion = f32[256,1024]{1,0:T(8,128)} fusion(f32[256,1024]{1,0:T(8,128)S(1)} %copy-done.2, f32[256,2048]{0,1:T(8,128)S(1)} %bitcast.52, f32[2048,1024]{1,0:T(8,128)S(1)} %bitcast.50), kind=kOutput, calls=%fused_computation.3 | convolution fusion | flops 3221487616 | bytes 12582912 | tf_op jit(solution)/shard_map/dot_general | solution.py:265
  (8 shorter events, 0.1 us)
Async XLA Ops:
  6.5 3.2 %copy-start = (f32[64,16,128]{2,1,0:T(8,128)S(1)}, f32[64,16,128]{2,1,0:T(8,128)}, u32[]{:S(2)}) copy-start(f32[64,16,128]{2,1,0:T(8,128)} %param.10) | copy-start | bytes 1572868
  6.5 145.0 %all-gather.3.cloned.1.call-start = ((), (), s32[]{:S(2)}) async-start(), calls=%async_computation | async-start | bytes 2162688 | tf_op jit(solution)/shard_map/all_gather | solution.py:260
  11.3 56.3 %copy-start.3 = (f32[256,32]{0,1:T(8,128)S(1)}, f32[256,32]{0,1:T(8,128)}, u32[]{:S(2)}) copy-start(f32[256,32]{0,1:T(8,128)} %param.9) | copy-start | bytes 98308
  73.9 79.7 %copy-start.2 = (f32[256,1024]{1,0:T(8,128)S(1)}, f32[256,1024]{1,0:T(8,128)}, u32[]{:S(2)}) copy-start(f32[256,1024]{1,0:T(8,128)} %param.8) | copy-start | bytes 3145732
  151.5 4.0 %copy-start.1 = (f32[8,256,1024]{2,1,0:T(8,128)S(1)}, f32[8,256,1024]{2,1,0:T(8,128)}, u32[]{:S(2)}) copy-start(f32[8,256,1024]{2,1,0:T(8,128)} %shard_map.65) | copy-start | bytes 25165828
Sparse Core Ops, SparseCore 0:
  69.1 80.5 all-gather.2

commit v15 on v13

--- a/solution.py
+++ b/solution.py
@@ -254,10 +254,10 @@
     nz = lax.axis_size("zl")
     gathered = row_gather(placed, nz)
     dense = gathered.reshape(-1, CT * width)
-    other = other_t.T
+    near = lax.all_gather(amplitudes, "xy", axis=0, tiled=False)
+    far = lax.all_gather(other_t.T, "xy", axis=0, tiled=False)
     lower = lax.axis_index("zh") == 0
-    pair = jnp.stack([jnp.where(lower, amplitudes, other), jnp.where(lower, other, amplitudes)])
-    blocks = lax.all_gather(pair, "xy", axis=0, tiled=False)
+    blocks = jnp.stack([jnp.where(lower, near, far), jnp.where(lower, far, near)], axis=1)
     rows, own_cols = amplitudes.shape
     amps = blocks.transpose(2, 1, 0, 3).reshape(rows, targets * own_cols)
     groups = gathered.shape[0]

time: 168 us -> 198 us (1.18)
  waiting for transfers between devices: 0.04 us -> 29.9 us
    all_gather x1 -> x2, waiting for transfers between devices: 0.02 us -> 29.2 us  [the longest x1 29.1 us: local(): far = lax.all_gather(other_t.T, 'xy', axis=0, tiled=False)]
  transfers between devices with their start and end apart: 1 -> 2, of which waited for: 0 -> 1; matrix products, arithmetic and copies ran while one was open for 3% -> 5% of each run, Pallas kernels for 46% -> 67%
where the time goes in v15:
time: 198 us; the launch traced here: 197 us
  Pallas kernels  133 us (67%)
  waiting for transfers between devices  29.9 us (15%)
  between operations  13.6 us (7%)
  local copies, waits for them, and re-layouts  7.95 us (4%)
  other arithmetic  7.52 us (4%)
  matrix products  5.8 us (3%)
    pallas_call x1, Pallas kernels, row_gather(): pl.pallas_call(functools.partial(gather_kernel, nz, RELAY_PARTS), out_sha...  77.9 us
    pallas_call x1, Pallas kernels, bulk_exchange(): pl.pallas_call(functools.partial(exchange_kernel, nb, nxy), out_shape=(ja...  54.7 us
    all_gather x1, waiting for transfers between devices, local(): far = lax.all_gather(other_t.T, 'xy', axis=0, tiled=False)  29.1 us
    dot_general x1, matrix products, local(): return residual_in + jnp.dot(amps, dense, precision=lax.Precision.HIGH)  5.11 us
  transfers between devices with their start and end apart: 2, of which 1 were waited for; matrix products, arithmetic and copies ran while one was open for 5% of the time, Pallas kernels for 67%

profile of v15, /device:TPU:6, one launch (start us, length us, event | category | flops | bytes accessed | tf_op | source)
XLA Modules:
  0.0 197.5 jit_solution(15790207744115745329)
XLA Ops:
  6.5 0.0 copy-start
  6.5 0.0 all-gather.5.cloned.1.call-start
  6.5 0.7 all-gather.5.cloned.1.call-update
  7.3 0.0 all-gather.7.cloned.1.call-start
  7.3 0.8 fusion.9
  8.1 0.1 reduce_window_sum.11
  8.2 0.8 select_reduce_fusion
  9.1 0.7 multiply_add_fusion.1
  9.7 0.2 fusion.1
  9.9 0.1 copy.22
  10.0 0.1 copy.21
  10.2 0.1 copy.20
  10.3 0.1 reshape.190
  10.4 0.1 copy.23
  10.5 0.0 copy-done
  10.5 0.8 gather_fusion
  11.3 0.7 fusion
  12.0 1.2 select_maximum_fusion.src_ref
  13.2 54.7 %shard_map.64 = (f32[64,33,128]{2,1,0:T(8,128)}, f32[32,256]{1,0:T(8,128)}) custom-call(f32[64,33,128]{2,1,0:T(8,128)} %select_maximum_fusion.src_ref, f32[32,256]{1,0:T(8,128)} %bitcast.63), custom_call_target="tpu_custom_call" | custom-call | tf_op jit(solution)/shard_map/pallas_call | solution.py:217
  67.9 0.0 all-gather.7.cloned.1.call-update
  68.0 1.3 slice.30
  69.3 1.1 convert_reduce_fusion
  70.3 0.1 convert_element_type.46
  70.5 0.2 reshape.192
  70.6 0.3 copy.27
  71.0 0.7 fusion.3
  71.7 1.2 copy.33
  72.8 77.9 %shard_map.65 = f32[8,256,1024]{2,1,0:T(8,128)} custom-call(f32[256,1024]{1,0:T(8,128)} %bitcast.56), custom_call_target="tpu_custom_call" | custom-call | tf_op jit(solution)/shard_map/pallas_call | solution.py:130
  150.8 0.0 all-gather.5.cloned.1.call-done
  150.8 29.1 %all-gather.7.cloned.1.call-done = f32[8192,32]{0,1:T(8,128)} async-done(((f32[256,32]{0,1:T(8,128)}), f32[8192,32]{0,1:T(8,128)}) %all-gather.7.cloned.1.call-update) | async-done | bytes 1048592 | tf_op jit(solution)/shard_map/all_gather | solution.py:258
  179.9 1.7 broadcast_select_fusion.1
  181.7 0.0 slice-start
  181.7 0.3 copy.29
  182.0 0.6 copy.24
  182.6 0.3 copy.30
  183.0 0.0 slice-start.1
  183.0 0.6 copy.25
  183.6 0.2 pad_maximum_fusion
  183.8 0.0 copy-start.1
  183.8 0.2 copy.26
  184.0 0.0 slice-done
  184.0 1.3 slice-done.1
  185.4 0.2 copy-done.1
  185.5 5.1 %convolution_add_fusion = f32[256,1024]{1,0:T(8,128)} fusion(f32[256,1024]{1,0:T(8,128)S(1)} %copy-done.1, f32[256,2048]{0,1:T(8,128)S(1)} %bitcast.53, f32[2048,1024]{1,0:T(8,128)S(1)} %bitcast.51), kind=kOutput, calls=%fused_computation.4 | convolution fusion | flops 3221487616 | bytes 12582912 | tf_op jit(solution)/shard_map/dot_general | solution.py:265
  (9 shorter events, 0.1 us)
Async XLA Ops:
  6.5 4.0 %copy-start = (f32[64,16,128]{2,1,0:T(8,128)S(1)}, f32[64,16,128]{2,1,0:T(8,128)}, u32[]{:S(2)}) copy-start(f32[64,16,128]{2,1,0:T(8,128)} %param.10) | copy-start | bytes 1572868
  6.5 144.3 %all-gather.5.cloned.1.call-start = ((), (), s32[]{:S(2)}) async-start(), calls=%async_computation | async-start | bytes 1081344 | tf_op jit(solution)/shard_map/all_gather | solution.py:257
  7.3 172.7 %all-gather.7.cloned.1.call-start = ((), (), s32[]{:S(2)}) async-start(), calls=%async_computation.1 | async-start | bytes 1081344 | tf_op jit(solution)/shard_map/all_gather | solution.py:258
  181.7 2.4 %slice-start = ((s8[8388608]{0:T(1024)(128)(4,1)}), s8[4194304]{0:T(1024)(128)(4,1)S(1)}, s32[]{:S(2)}) async-start(s8[8388608]{0:T(1024)(128)(4,1)} %bitcast.49), calls=%async_computation.2 | async-start | bytes 8388608
  183.0 2.4 %slice-start.1 = ((s8[8388608]{0:T(1024)(128)(4,1)}), s8[4194304]{0:T(1024)(128)(4,1)S(1)}, s32[]{:S(2)}) async-start(s8[8388608]{0:T(1024)(128)(4,1)} %bitcast.49), calls=%async_computation.3 | async-start | bytes 8388608
  183.8 1.7 copy-start.1
Sparse Core Ops, SparseCore 0:
  10.4 90.9 all-gather.4
  104.4 75.4 all-gather.6

commit v16 on v13

--- a/solution.py
+++ b/solution.py
@@ -63,14 +63,14 @@
         rows = pl.ds(q * piece, piece)
         return pltpu.make_async_remote_copy(
             src_ref=src.at[rows],
-            dst_ref=out_ref.at[slot, rows],
+            dst_ref=out_ref.at[rows, slot],
             send_sem=send_sem.at[slot, q, kind],
             recv_sem=recv_sem.at[slot, q],
             device_id=dev,
             device_id_type=MESH,
         )
 
-    mine = pltpu.make_async_copy(src_ref, out_ref.at[own], local_sem)
+    mine = pltpu.make_async_copy(src_ref, out_ref.at[:, own], local_sem)
     mine.start()
     for q in range(parts):
         copy(src_ref, own, 0, partner, q).start()
@@ -88,48 +88,48 @@
             @pl.when(zl - d >= 0)
             def _():
                 s = (zl - d) * 2 + c
-                copy(out_ref.at[s], s, 0, partner, q).wait_recv()
-                copy(out_ref.at[s], s, 0, partner, q).start()
+                copy(out_ref.at[:, s], s, 0, partner, q).wait_recv()
+                copy(out_ref.at[:, s], s, 0, partner, q).start()
 
                 @pl.when(has_right)
                 def _():
-                    copy(out_ref.at[s], s, 2, right, q).start()
+                    copy(out_ref.at[:, s], s, 2, right, q).start()
 
             @pl.when(zl + d <= nz - 1)
             def _():
                 s = (zl + d) * 2 + c
-                copy(out_ref.at[s], s, 0, partner, q).wait_recv()
-                copy(out_ref.at[s], s, 0, partner, q).start()
+                copy(out_ref.at[:, s], s, 0, partner, q).wait_recv()
+                copy(out_ref.at[:, s], s, 0, partner, q).start()
 
                 @pl.when(has_left)
                 def _():
-                    copy(out_ref.at[s], s, 1, left, q).start()
+                    copy(out_ref.at[:, s], s, 1, left, q).start()
 
     for z in range(nz):
         s = z * 2 + (1 - c)
         for q in range(parts):
-            copy(out_ref.at[s], s, 0, partner, q).wait_recv()
+            copy(out_ref.at[:, s], s, 0, partner, q).wait_recv()
 
     mine.wait()
     for z in range(nz):
         s = z * 2 + c
         for q in range(parts):
-            copy(out_ref.at[s], s, 0, partner, q).wait_send()
+            copy(out_ref.at[:, s], s, 0, partner, q).wait_send()
 
             @pl.when(has_left & (z >= zl))
             def _():
-                copy(out_ref.at[s], s, 1, left, q).wait_send()
+                copy(out_ref.at[:, s], s, 1, left, q).wait_send()
 
             @pl.when(has_right & (z <= zl))
             def _():
-                copy(out_ref.at[s], s, 2, right, q).wait_send()
+                copy(out_ref.at[:, s], s, 2, right, q).wait_send()
 
 
 def row_gather(placed, nz):
     groups = 2 * nz
     return pl.pallas_call(
         functools.partial(gather_kernel, nz, RELAY_PARTS),
-        out_shape=jax.ShapeDtypeStruct((groups,) + placed.shape, placed.dtype),
+        out_shape=jax.ShapeDtypeStruct(placed.shape[:1] + (groups,) + placed.shape[1:], placed.dtype),
         in_specs=[pl.BlockSpec(memory_space=pltpu.VMEM)],
         out_specs=pl.BlockSpec(memory_space=pltpu.VMEM),
         scratch_shapes=[
@@ -250,7 +250,7 @@
     arrived = arrived[:, : SLOT * height, :].reshape(targets * SLOT, height * width)
     table = (position[None, :] == jnp.arange(KT * CT, dtype=jnp.int32)[:, None]).astype(jnp.float32)
     placed = jnp.dot(table, arrived, precision=lax.Precision.HIGHEST)
-    placed = placed.reshape(KT, CT, height, width).transpose(0, 2, 1, 3).reshape(KT * height, CT * width)
+    placed = placed.reshape(KT, CT, height, width).transpose(0, 2, 1, 3).reshape(KT, height, CT * width)
     nz = lax.axis_size("zl")
     gathered = row_gather(placed, nz)
     dense = gathered.reshape(-1, CT * width)
@@ -260,8 +260,6 @@
     blocks = lax.all_gather(pair, "xy", axis=0, tiled=False)
     rows, own_cols = amplitudes.shape
     amps = blocks.transpose(2, 1, 0, 3).reshape(rows, targets * own_cols)
-    groups = gathered.shape[0]
-    amps = amps.reshape(rows, KT, groups, height).transpose(0, 2, 1, 3).reshape(rows, -1)
     return residual_in + jnp.dot(amps, dense, precision=lax.Precision.HIGH)
 
 

time: 168 us -> 168 us (level)
  matrix products: 5.8 us -> 8 us
  local copies, waits for them, and re-layouts: 8.38 us -> 6.29 us
    unnamed x9 -> x6, local copies, waits for them, and re-layouts: 3.09 us -> 0.02 us
    dot_general x1, matrix products: 5.11 us -> 7.31 us  [local(): return residual_in + jnp.dot(amps, dense, precision=lax.Precision.HIGH)]
where the time goes in v16:
time: 168 us; the launch traced here: 167 us
  Pallas kernels  132 us (79%)
  between operations  13.6 us (8%)
  matrix products  8 us (5%)
  other arithmetic  6.97 us (4%)
  local copies, waits for them, and re-layouts  6.29 us (4%)
    pallas_call x1, Pallas kernels, row_gather(): pl.pallas_call(functools.partial(gather_kernel, nz, RELAY_PARTS), out_sha...  77.3 us
    pallas_call x1, Pallas kernels, bulk_exchange(): pl.pallas_call(functools.partial(exchange_kernel, nb, nxy), out_shape=(ja...  55.1 us
    dot_general x1, matrix products, local(): return residual_in + jnp.dot(amps, dense, precision=lax.Precision.HIGH)  7.31 us
  transfers between devices with their start and end apart: 1, of which 0 were waited for; matrix products, arithmetic and copies ran while one was open for 3% of the time, Pallas kernels for 46%

profile of v16, /device:TPU:6, one launch (start us, length us, event | category | flops | bytes accessed | tf_op | source)
XLA Modules:
  0.0 167.3 jit_solution(13141105568674693085)
XLA Ops:
  6.5 0.0 copy-start
  6.5 0.0 all-gather.3.cloned.1.call-start
  6.5 0.8 fusion.10
  7.3 0.1 reduce_window_sum.11
  7.4 0.8 select_reduce_fusion
  8.3 0.7 multiply_add_fusion.1
  9.0 0.2 fusion.1
  9.2 0.1 copy.31
  9.3 0.1 copy.30
  9.4 0.1 copy.29
  9.5 0.1 reshape.190
  9.7 0.1 copy.32
  9.8 0.0 copy-done
  9.8 0.8 gather_fusion
  10.5 0.7 fusion
  11.3 0.0 copy-start.2
  11.3 1.2 select_maximum_fusion.src_ref
  12.5 55.1 %shard_map.64 = (f32[64,33,128]{2,1,0:T(8,128)}, f32[32,256]{1,0:T(8,128)}) custom-call(f32[64,33,128]{2,1,0:T(8,128)} %select_maximum_fusion.src_ref, f32[32,256]{1,0:T(8,128)} %bitcast.51), custom_call_target="tpu_custom_call" | custom-call | tf_op jit(solution)/shard_map/pallas_call | solution.py:217
  67.6 0.0 copy-done.2
  67.6 0.8 fusion.5
  68.4 0.6 pad_maximum_fusion
  69.0 0.0 all-gather.3.cloned.1.call-update
  69.0 1.3 slice.30
  70.3 1.1 convert_reduce_fusion
  71.4 0.1 convert_element_type.46
  71.5 0.2 reshape.192
  71.7 0.3 copy.34
  72.0 0.7 convolution_bitcast_fusion
  72.7 1.1 reshape.193.src_ref
  73.8 77.3 %shard_map.65 = f32[16,8,16,1024]{3,2,1,0:T(8,128)} custom-call(f32[16,16,1024]{2,1,0:T(8,128)} %reshape.193.src_ref), custom_call_target="tpu_custom_call" | custom-call | tf_op jit(solution)/shard_map/pallas_call | solution.py:130
  151.1 0.0 all-gather.3.cloned.1.call-done
  151.2 0.0 copy-start.1
  151.2 1.9 %copy.33 = f32[256,2,32,32]{0,3,2,1:T(8,128)S(1)} copy(f32[256,2,32,32]{0,3,1,2:T(8,128)} %bitcast.50) | data formatting | bytes 4194304 | tf_op jit(solution)/shard_map/transpose | solution.py:262
  153.1 0.0 copy-done.1
  153.1 7.3 %convolution_add_fusion = f32[256,1024]{1,0:T(8,128)} fusion(f32[256,1024]{1,0:T(8,128)S(1)} %copy-done.1, f32[256,2048]{0,1:T(8,128)S(1)} %bitcast.46, f32[2048,1024]{1,0:T(8,128)} %bitcast.45), kind=kOutput, calls=%fused_computation.4 | convolution fusion | flops 3221487616 | bytes 12582912 | tf_op jit(solution)/shard_map/dot_general | solution.py:263
  (8 shorter events, 0.1 us)
Async XLA Ops:
  6.5 3.2 %copy-start = (f32[64,16,128]{2,1,0:T(8,128)S(1)}, f32[64,16,128]{2,1,0:T(8,128)}, u32[]{:S(2)}) copy-start(f32[64,16,128]{2,1,0:T(8,128)} %param.10) | copy-start | bytes 1572868
  6.5 144.6 %all-gather.3.cloned.1.call-start = ((), (), s32[]{:S(2)}) async-start(), calls=%async_computation | async-start | bytes 2162688 | tf_op jit(solution)/shard_map/all_gather | solution.py:260
  11.3 56.3 %copy-start.2 = (f32[256,32]{0,1:T(8,128)S(1)}, f32[256,32]{0,1:T(8,128)}, u32[]{:S(2)}) copy-start(f32[256,32]{0,1:T(8,128)} %param.9) | copy-start | bytes 98308
  151.2 1.9 %copy-start.1 = (f32[256,1024]{1,0:T(8,128)S(1)}, f32[256,1024]{1,0:T(8,128)}, u32[]{:S(2)}) copy-start(f32[256,1024]{1,0:T(8,128)} %param.8) | copy-start | bytes 3145732
Sparse Core Ops, SparseCore 0:
  69.1 80.5 all-gather.2

commit v17 on v13

--- a/solution.py
+++ b/solution.py
@@ -173,7 +173,8 @@
         )
 
     def send(p, carry):
-        copy(p, lax.rem(me + p, nb)).start()
+        step = lax.rem(p + nb // 2 - 2, nb - 1) + 1
+        copy(step, lax.rem(me + step, nb)).start()
         return carry
 
     lax.fori_loop(1, nb, send, 0)

time: 168 us -> 170 us (1.012)
  transfers between devices with their start and end apart: 1 -> 1, of which waited for: 0 -> 1; matrix products, arithmetic and copies ran while one was open for 3% -> 3% of each run, Pallas kernels for 46% -> 46%
where the time goes in v17:
time: 170 us; the launch traced here: 169 us
  Pallas kernels  133 us (78%)
  between operations  13.6 us (8%)
  local copies, waits for them, and re-layouts  8.39 us (5%)
  other arithmetic  6.97 us (4%)
  matrix products  5.8 us (3%)
    pallas_call x1, Pallas kernels, row_gather(): pl.pallas_call(functools.partial(gather_kernel, nz, RELAY_PARTS), out_sha...  77.1 us
    pallas_call x1, Pallas kernels, bulk_exchange(): pl.pallas_call(functools.partial(exchange_kernel, nb, nxy), out_shape=(ja...  55.6 us
    dot_general x1, matrix products, local(): return residual_in + jnp.dot(amps, dense, precision=lax.Precision.HIGH)  5.11 us
  transfers between devices with their start and end apart: 1, of which 1 were waited for; matrix products, arithmetic and copies ran while one was open for 3% of the time, Pallas kernels for 46%

profile of v17, /device:TPU:6, one launch (start us, length us, event | category | flops | bytes accessed | tf_op | source)
XLA Modules:
  0.0 168.8 jit_solution(6889981208213019849)
XLA Ops:
  6.5 0.0 copy-start
  6.5 0.0 all-gather.3.cloned.1.call-start
  6.5 0.8 fusion.11
  7.3 0.1 reduce_window_sum.11
  7.4 0.8 select_reduce_fusion
  8.3 0.7 multiply_add_fusion.1
  9.0 0.2 fusion.1
  9.2 0.1 copy.34
  9.3 0.1 copy.33
  9.4 0.1 copy.32
  9.5 0.1 reshape.190
  9.7 0.1 copy.35
  9.8 0.0 copy-done
  9.8 0.8 gather_fusion
  10.5 0.7 fusion
  11.3 0.0 copy-start.3
  11.3 1.2 select_maximum_fusion.src_ref
  12.5 55.6 %shard_map.64 = (f32[64,33,128]{2,1,0:T(8,128)}, f32[32,256]{1,0:T(8,128)}) custom-call(f32[64,33,128]{2,1,0:T(8,128)} %select_maximum_fusion.src_ref, f32[32,256]{1,0:T(8,128)} %bitcast.59), custom_call_target="tpu_custom_call" | custom-call | tf_op jit(solution)/shard_map/pallas_call | solution.py:218
  68.0 0.0 copy-done.3
  68.0 0.8 fusion.6
  68.8 0.6 pad_maximum_fusion
  69.4 0.0 all-gather.3.cloned.1.call-update
  69.5 1.3 slice.30
  70.8 1.1 convert_reduce_fusion
  71.8 0.1 convert_element_type.46
  72.0 0.2 reshape.192
  72.1 0.3 copy.38
  72.5 0.7 fusion.3
  73.2 1.2 copy.42
  74.3 0.0 copy-start.2
  74.3 77.1 %shard_map.65 = f32[8,256,1024]{2,1,0:T(8,128)} custom-call(f32[256,1024]{1,0:T(8,128)} %bitcast.53), custom_call_target="tpu_custom_call" | custom-call | tf_op jit(solution)/shard_map/pallas_call | solution.py:130
  151.4 1.4 all-gather.3.cloned.1.call-done
  152.8 0.0 copy-start.1
  152.8 1.9 %copy.36 = f32[256,2,32,32]{0,3,2,1:T(8,128)S(1)} copy(f32[256,2,32,32]{0,3,1,2:T(8,128)} %bitcast.58) | data formatting | bytes 4194304 | tf_op jit(solution)/shard_map/transpose | solution.py:263
  154.7 0.2 copy.37
  154.9 0.0 copy-done.2
  154.9 1.9 %copy-done.1 = f32[8,256,1024]{2,1,0:T(8,128)S(1)} copy-done((f32[8,256,1024]{2,1,0:T(8,128)S(1)}, f32[8,256,1024]{2,1,0:T(8,128)}, u32[]{:S(2)}) %copy-start.1) | copy-done | bytes 8388632
  156.8 5.1 %convolution_add_fusion = f32[256,1024]{1,0:T(8,128)} fusion(f32[256,1024]{1,0:T(8,128)S(1)} %copy-done.2, f32[256,2048]{0,1:T(8,128)S(1)} %bitcast.52, f32[2048,1024]{1,0:T(8,128)S(1)} %bitcast.50), kind=kOutput, calls=%fused_computation.3 | convolution fusion | flops 3221487616 | bytes 12582912 | tf_op jit(solution)/shard_map/dot_general | solution.py:266
  (8 shorter events, 0.1 us)
Async XLA Ops:
  6.5 3.2 %copy-start = (f32[64,16,128]{2,1,0:T(8,128)S(1)}, f32[64,16,128]{2,1,0:T(8,128)}, u32[]{:S(2)}) copy-start(f32[64,16,128]{2,1,0:T(8,128)} %param.10) | copy-start | bytes 1572868
  6.5 146.3 %all-gather.3.cloned.1.call-start = ((), (), s32[]{:S(2)}) async-start(), calls=%async_computation | async-start | bytes 2162688 | tf_op jit(solution)/shard_map/all_gather | solution.py:261
  11.3 56.8 %copy-start.3 = (f32[256,32]{0,1:T(8,128)S(1)}, f32[256,32]{0,1:T(8,128)}, u32[]{:S(2)}) copy-start(f32[256,32]{0,1:T(8,128)} %param.9) | copy-start | bytes 98308
  74.3 80.6 %copy-start.2 = (f32[256,1024]{1,0:T(8,128)S(1)}, f32[256,1024]{1,0:T(8,128)}, u32[]{:S(2)}) copy-start(f32[256,1024]{1,0:T(8,128)} %param.8) | copy-start | bytes 3145732
  152.8 4.0 %copy-start.1 = (f32[8,256,1024]{2,1,0:T(8,128)S(1)}, f32[8,256,1024]{2,1,0:T(8,128)}, u32[]{:S(2)}) copy-start(f32[8,256,1024]{2,1,0:T(8,128)} %shard_map.65) | copy-start | bytes 25165828
Sparse Core Ops, SparseCore 0:
  69.6 83.1 all-gather.2
